TPU v7x, 256 devices: a whole 4x4x8 slice. The times are simulated.
256 devices in a mesh: epoch: 8 (over z_lo, core), prow: 8 (over z_hi, x), pcol: 4 (over y).
Axes of the slice: x: 4, y: 4, z: 8 (z_hi: 2, z_lo: 4; z = z_hi * 4 + z_lo), core: 2. Of those that a mesh axis runs over, the one named last changes fastest.
Arguments:
- steps: int32 [2, 16384], P(None, 'epoch'), may hold values from 0 to 47
- harmonic: int32 [4096], replicated, may hold values from 0 to 4095, each once
- col_scale: float32 [4096], replicated, may hold values from 0.3 to 3
- taps: float32 [256], replicated, may hold values from -0.375 to 0.375
- ridge: float32 [4096], P(('epoch', 'prow')), may hold values from 0.1 to 1
Outputs:
- panel: float32 [4096, 256], P(('epoch', 'prow'))
- schur: float32 [4096, 4096], P(('epoch', 'prow'), 'pcol')
Inputs may be any that keep to these rules, and one draw needn't show every extreme that they name: `harmonic`: each of 0 to 4095 once.
All inputs are finite; a program needn't handle non-finite values.
Results may differ from a plain program's by a relative error of at most 0.0028.
Values may be sent and summed in bfloat16 or wider, within the bound.
A program may use at most 64 MiB of HBM per device.

v0:
```python
import math

import jax
import jax.numpy as jnp
from jax import lax
from jax.sharding import Mesh
from jax.sharding import PartitionSpec as P

B = 256
EPOCH = ("epoch_0", "epoch_1")
EPOCH_PROW = ("epoch_0", "epoch_1", "prow")


phase_count = 4096
angle_step = 2.0 * math.pi / 4096.0


def from_everyone(x, axis):
    count = lax.axis_size(axis)
    return lax.all_to_all(jnp.broadcast_to(x[None], (count, *x.shape)), axis, 0, 0, tiled=True)


def joined_by_halves(pieces, combine):
    while len(jax.tree.leaves(pieces)[0]) > 1:
        pieces = jax.vmap(combine)(*(pieces[side::2] for side in (0, 1)))
    return pieces[0]


def entering(x, axis, combine, identity):
    count, position = (lax.axis_size(axis), lax.axis_index(axis))
    passed = jnp.arange(count) < position

    def kept(part, zero, own):
        part = jnp.where(
            passed.reshape(-1, *(1 for _ in own.shape)), part, jnp.asarray(zero, own.dtype)
        )
        return part

    pieces = from_everyone(x, axis)
    return joined_by_halves(kept(pieces, identity, x), combine)


def shifted(x, axis, by):
    count = lax.axis_size(axis)
    pairs = [(i, i + by) for i in range(count) if 0 <= i + by < count]
    return lax.ppermute(x, axis, pairs)


def sum_in_order(tiles, axes, order):
    inside = tiles.shape[1:]
    tiles = tiles.reshape(*(lax.axis_size(a) for a in axes), *inside)
    tiles = jnp.moveaxis(tiles, order, range(len(axes))).reshape(-1, *inside)
    for k in order:
        tiles = lax.psum_scatter(tiles, axes[k], scatter_dimension=0, tiled=True)
    return tiles[0]


def in_blocks(x, dim, count):
    dims = x.shape
    tiles = x.reshape(*dims[:dim], count, dims[dim] // count, *dims[dim + 1 :])
    return jnp.moveaxis(tiles, dim, 0)


def summed_rows_2(x, axes, order, dim):
    count = lax.axis_size(axes)
    return sum_in_order(in_blocks(x, dim, count), axes, order)


def picked(x, axis, root):
    return lax.dynamic_index_in_dim(lax.all_gather(x, axis), root, 0, keepdims=False)


def joined_along(tiles, dim):
    tiles = jnp.moveaxis(tiles, 0, dim)
    dims = tiles.shape
    return tiles.reshape(*dims[:dim], dims[dim] * dims[dim + 1], *dims[dim + 2 :])


def gather_directly(x, axis, dim):
    tiles = from_everyone(x, axis)
    return joined_along(tiles, dim)


def toeplitz_pair(taps):
    count = taps.shape[0]
    pattern = jnp.concatenate(
        [jnp.zeros((1,), jnp.float32), taps[::-1], jnp.zeros((count,), jnp.float32)]
    )
    full = (
        jnp.tile(pattern, count)[: 2 * count * count].reshape(count, 2 * count).astype(jnp.bfloat16)
    )
    return (full[:, :count], full[:, count:])


def harmonic_design(phase_first, phase_second, orders, degrees, scales):
    indices = (
        phase_first[:, None] * orders[None, :] + phase_second[:, None] * degrees[None, :]
    ) % phase_count
    angle = indices.astype(jnp.float32) * angle_step
    return (jnp.cos(angle) + jnp.sin(angle)) * scales[None, :]


def add_phase(earlier, later):
    return (earlier + later) % phase_count


def on_device(steps, harmonic, col_scale, taps, ridge):
    epochs_here = steps.shape[1]
    count = taps.shape[0]
    params = harmonic.shape[0]
    n_epoch = lax.axis_size(EPOCH)
    n_row = lax.axis_size("prow")
    n_col = lax.axis_size("pcol")
    row_block = params // (n_epoch * n_row)
    col_block = params // n_col
    epoch_id = lax.axis_index(EPOCH)
    row_id = lax.axis_index("prow")
    col_id = lax.axis_index("pcol")
    row_harm = lax.dynamic_slice_in_dim(
        harmonic.reshape(n_epoch, n_row, row_block), row_id, 1, 1
    ).reshape(-1)
    row_scale = lax.dynamic_slice_in_dim(
        col_scale.reshape(n_epoch, n_row, row_block), row_id, 1, 1
    ).reshape(-1)
    col_harm = lax.dynamic_slice_in_dim(harmonic, col_id * col_block, col_block)
    col_scales = lax.dynamic_slice_in_dim(col_scale, col_id * col_block, col_block)
    harm = jnp.concatenate([row_harm, col_harm])
    scales = jnp.concatenate([row_scale, col_scales])
    orders = harm // 64
    degrees = harm % 64
    running = jnp.cumsum(steps, axis=1)
    totals = running[:, -1] % phase_count
    base = entering(totals, EPOCH, add_phase, jnp.zeros((2,), jnp.int32))
    phase = (base[:, None] + running) % phase_count
    design = harmonic_design(phase[0], phase[1], orders, degrees, scales).astype(jnp.bfloat16)
    carried = shifted(steps[:, epochs_here - count :], EPOCH, 1)
    partial_sums = jnp.cumsum(carried, axis=1)
    earlier_phase = (base[:, None] - partial_sums[:, -1:] + partial_sums) % phase_count
    present = (epoch_id > 0).astype(jnp.float32)
    tail = (
        harmonic_design(earlier_phase[0], earlier_phase[1], orders, degrees, scales) * present
    ).astype(jnp.bfloat16)
    joined = jnp.concatenate([tail, design], axis=0)
    blocks = epochs_here // count
    width = harm.shape[0]
    earlier_rows = joined[:epochs_here].reshape(blocks, count, width)
    current_rows = joined[count:].reshape(blocks, count, width)
    lower_part, upper_part = toeplitz_pair(taps)
    filtered = jnp.einsum(
        "ij,bjc->bic", lower_part, earlier_rows, preferred_element_type=jnp.float32
    )
    filtered = filtered + jnp.einsum(
        "ij,bjc->bic", upper_part, current_rows, preferred_element_type=jnp.float32
    )
    filtered = filtered.reshape(epochs_here, width).astype(jnp.bfloat16)
    row_cols = filtered[:, : params // n_row]
    col_cols = filtered[:, params // n_row :]
    scale_total = 1.0 / (epochs_here * n_epoch)
    product = lax.dot_general(
        row_cols, col_cols, (((0,), (0,)), ((), ())), preferred_element_type=jnp.float32
    )
    normal = summed_rows_2(product * scale_total, EPOCH, (1, 0), 0)
    first_row = (epoch_id * n_row + row_id) * row_block
    global_rows = first_row + jnp.arange(row_block, dtype=jnp.int32)
    global_cols = col_id * col_block + jnp.arange(col_block, dtype=jnp.int32)
    normal = normal + jnp.where(
        global_rows[:, None] == global_cols[None, :], ridge[:, None], jnp.float32(0.0)
    )
    leading_cols = normal[:, :B]
    spread = picked(leading_cols, "pcol", 0)
    group_rows = gather_directly(spread, "prow", 0)
    lead_rows = picked(group_rows[:B], EPOCH, 0)
    per_col = n_epoch // n_col
    col_slabs = []
    for offset in range(per_col):
        col_slabs.append(picked(group_rows, EPOCH, col_id * per_col + offset))
    col_slab = jnp.concatenate(col_slabs, axis=0)
    leading = jnp.linalg.cholesky(lead_rows)
    own_rows = jax.scipy.linalg.solve_triangular(leading, spread.T, lower=True).T
    col_rows = jax.scipy.linalg.solve_triangular(leading, col_slab.T, lower=True).T
    schur = normal - jnp.dot(
        own_rows, col_rows.T, precision=lax.Precision.HIGHEST, preferred_element_type=jnp.float32
    )
    return (own_rows, schur)


def solution(mesh):
    split = Mesh(
        mesh.devices.reshape(4, 2, mesh.shape["prow"], mesh.shape["pcol"]),
        ("epoch_0", "epoch_1", "prow", "pcol"),
    )
    return jax.shard_map(
        on_device,
        mesh=split,
        in_specs=(P(None, EPOCH), P(), P(), P(), P(EPOCH_PROW)),
        out_specs=(P(EPOCH_PROW, None), P(EPOCH_PROW, "pcol")),
        check_vma=False,
    )
```

profile of v0, /device:TPU:1, one launch (start us, length us, event | category | flops | bytes accessed | tf_op | source)
XLA Modules:
  0.0 346.5 jit_solution(13144682526733546442)
XLA Ops:
  7.2 0.7 copy.40
  7.9 0.6 reduce-window.14
  9.1 0.6 broadcast_in_dim.34
  9.7 7.4 %all-to-all-start = ((s32[8,1,2]{2,1,0:T(1,128)}), s32[8,1,2]{2,1,0:T(1,128)S(1)}, u32[]{:S(2)}, u32[]{:S(2)}) async-start(s32[8,1,2]{2,1,0:T(1,128)} %broadcast_in_dim.34), calls=%async_computation | async-start | bytes 8192 | tf_op jit(solution)/shard_map/all_to_all | solution.py:20
  17.1 0.7 slice.152
  17.8 3.5 %collective-permute-start = (s32[2,256]{1,0:T(2,128)S(1)}, s32[2,256]{1,0:T(2,128)S(1)}, u32[]{:S(2)}, u32[]{:S(2)}) collective-permute-start(s32[2,256]{1,0:T(2,128)S(1)} %slice.152), channel_id=1, source_target_pairs={{0,32},{32,64},{64,96},{96,128},{128,160},{160,192},{192,224},{1,3... | collective-permute-start | bytes 6152 | tf_op jit(solution)/shard_map/ppermute | solution.py:46
  21.3 0.8 reshape.265
  22.1 0.7 dynamic_slice.28
  22.8 0.7 dynamic_slice.30
  23.5 0.8 reshape.266
  24.5 0.8 rev.3
  25.4 0.6 tile.11
  27.1 53.6 %multiply_convert_fusion.1 = bf16[2048,1536]{1,0:T(8,128)(2,1)} fusion(f32[1536]{0:T(1024)S(1)} %pad_maximum_fusion.3, s32[1536]{0:T(1024)S(1)} %get-tuple-element.33, s32[2048]{0:T(1024)S(1)} %bitcast.115, s32[1536]{0:T(1024)S(1)} %get-tuple-element.32, s32[2048]{0:T(1024)S(1)} %bitcast.116), kind=kLoop, calls=%fused_computation.16 | loop fusion | flops 59768832 | bytes 6326272 | tf_op jit(solution)/shard_map/convert_element_type | solution.py:135
  80.8 0.6 reduce-window.16
  82.1 6.8 %multiply_convert_fusion.3 = bf16[256,1536]{1,0:T(8,128)(2,1)S(1)} fusion(f32[]{:T(128)S(6)} %convert_element_type.35, f32[1536]{0:T(1024)S(1)} %pad_maximum_fusion.3, s32[1536]{0:T(1024)S(1)} %get-tuple-element.33, s32[256]{0:T(256)S(1)} %bitcast.121, s32[1536]{0:T(1024)S(1)} %get-tuple-element.32, s32[256]{0:T(256)S(1)} %bitcast.120), kind=kLoop, calls=%fused_computation.36 | loop fusion | flops 7864320 | bytes 806916 | tf_op jit(solution)/shard_map/convert_element_type | solution.py:142
  89.0 3.0 pad_maximum_fusion
  91.9 1.8 fusion.32
  93.7 53.7 %add_convert_fusion = bf16[8,1536,256]{1,2,0:T(8,128)(2,1)S(1)} fusion(f32[8,1536,256]{1,2,0:T(8,128)S(1)} %fusion.32, f32[1536]{0:T(1024)S(1)} %pad_maximum_fusion.3, s32[1536]{0:T(1024)S(1)} %get-tuple-element.33, s32[8,256]{1,0:T(8,128)S(1)} %mul.179, s32[1536]{0:T(1024)S(1)} %get-tuple-element.32, s32[8,256]{1,0:T(8,128)S(1)} %mul.175, ...), kind=kOutput, calls=%fused_computation.14 | convolution fusion | flops 1676673024 | bytes 19040256 | tf_op jit(solution)/shard_map/ij,bjc->bic/dot_general | solution.py:152
  147.4 2.3 fusion.21
  149.8 1.6 copy.20
  151.5 15.2 %reduce-scatter.3.cloned.1.call-done = f32[4,64,1024]{2,1,0:T(8,128)} async-done(((f32[8,64,1024]{2,1,0:T(8,128)}), f32[4,64,1024]{2,1,0:T(8,128)}) %reduce-scatter.3.cloned.1.call-update) | async-done | bytes 1048592 | tf_op jit(solution)/shard_map/reduce_scatter | solution.py:54
  166.8 35.8 %reduce-scatter.5.cloned.1.call-done = f32[1,64,1024]{2,1,0:T(8,128)} async-done(((f32[4,64,1024]{2,1,0:T(8,128)}), f32[1,64,1024]{2,1,0:T(8,128)}) %reduce-scatter.5.cloned.1.call-update) | async-done | bytes 262160 | tf_op jit(solution)/shard_map/reduce_scatter | solution.py:54
  202.6 1.0 bitcast_add_fusion.1
  203.7 10.6 %all-gather = f32[256,256]{1,0:T(8,128)S(1)} all-gather(f32[64,256]{1,0:T(8,128)S(1)} %slice.193), channel_id=2, replica_groups=mesh['epoch_0'=4,'epoch_1'=2,'prow'=8,'pcol'=4] {'pcol'}, dimensions={0}, use_global_device_ids=true | all-gather | bytes 327680 | tf_op jit(solution)/shard_map/all_gather | solution.py:70
  214.3 18.1 %all_to_all.14 = f32[8,64,256]{2,1,0:T(8,128)S(1)} all-to-all(f32[8,64,256]{2,1,0:T(8,128)S(1)} %broadcast_in_dim.59), channel_id=1, replica_groups=mesh['epoch_0'=4,'epoch_1'=2,'prow'=8,'pcol'=4] {'prow'}, dimensions={0} | all-to-all | bytes 1048576 | tf_op jit(solution)/shard_map/all_to_all | solution.py:20
  232.4 0.8 slice.195
  233.2 0.3 all-gather.6.cloned.1.call-start
  233.5 0.3 all-gather.6.cloned.1.call-update
  233.8 37.9 %all-gather.4.cloned.1.call-done = f32[8,256,256]{2,1,0:T(8,128)} async-done(((f32[1,256,256]{2,1,0:T(8,128)}), f32[8,256,256]{2,1,0:T(8,128)}) %all-gather.4.cloned.1.call-update) | async-done | bytes 2097168 | tf_op jit(solution)/shard_map/all_gather | solution.py:70
  271.7 1.0 dynamic_slice.35
  272.8 1.0 fusion.31
  273.8 11.7 %cholesky.50 = f32[128,128]{1,0:T(8,128)S(1)} custom-call(f32[128,128]{1,0:T(8,128)S(1)} %cholesky.118), custom_call_target="Cholesky" | custom-call | tf_op jit(solution)/shard_map/jit(cholesky)/cholesky | solution.py:178
  285.6 9.8 %custom-call.18 = f32[1,128,128]{1,2,0:T(8,128)S(1)} custom-call(f32[1,128,128]{2,1,0:T(8,128)S(1)} %get-tuple-element.29), custom_call_target="InvertDiagBlocksLowerTriangular" | custom-call | tf_op jit(solution)/shard_map/jit(cholesky)/cholesky | solution.py:178
  295.6 0.3 convolution_subtract_fusion.2
  295.9 11.7 %cholesky.105 = f32[128,128]{1,0:T(8,128)S(1)} custom-call(f32[128,128]{1,0:T(8,128)S(1)} %convolution_subtract_fusion.2), custom_call_target="Cholesky" | custom-call | tf_op jit(solution)/shard_map/jit(cholesky)/cholesky | solution.py:178
  307.6 0.6 compare_reduce_fusion
  309.7 4.2 %while.1 = (s32[]{:T(128)}, f32[256,256]{1,0:T(8,128)S(1)}, s32[2,2]{1,0:T(2,128)S(1)}, f32[2,128,128]{2,1,0:T(8,128)S(1)}, s32[]{:T(128)}) while((s32[]{:T(128)}, f32[256,256]{1,0:T(8,128)S(1)}, s32[2,2]{1,0:T(2,128)S(1)}, f32[2,128,128]{2,1,0:T(8,128)S(1)}, s32[]{:T(128)}) %tuple.34), condition=%wide.while_cond, body=%wide.while_body.sunk | while | flops 2 | bytes 131181 | solution.py:179
  309.9 0.6 fusion.69
  310.5 1.4 bitcast_dynamic-update-slice_fusion.2
  311.9 0.6 fusion.69
  312.5 1.4 bitcast_dynamic-update-slice_fusion.2
  313.9 19.7 %custom-call.19 = f32[2,128,128]{1,2,0:T(8,128)S(1)} custom-call(f32[2,128,128]{2,1,0:T(8,128)S(1)} %get-tuple-element.9), custom_call_target="InvertDiagBlocksLowerTriangular" | custom-call | tf_op jit(solution)/shard_map/jit(_solve_triangular)/triangular_solve | solution.py:179
  334.2 0.6 fusion.41
  334.8 1.3 constant_dynamic-slice_fusion.2
  336.6 0.6 fusion.29
  337.2 0.6 convolution_subtract_fusion
  337.8 0.6 fusion.37
  338.5 1.5 convolution_subtract_fusion.1
  (79 shorter events, 4.6 us)
Async XLA Ops:
  9.7 16.5 %all-to-all-start = ((s32[8,1,2]{2,1,0:T(1,128)}), s32[8,1,2]{2,1,0:T(1,128)S(1)}, u32[]{:S(2)}, u32[]{:S(2)}) async-start(s32[8,1,2]{2,1,0:T(1,128)} %broadcast_in_dim.34), calls=%async_computation | async-start | bytes 8192 | tf_op jit(solution)/shard_map/all_to_all | solution.py:20
  17.1 149.6 %reduce-scatter.3.cloned.1.call-start = ((), (), s32[]{:S(2)}) async-start(), calls=%async_computation.4 | async-start | bytes 3145728 | tf_op jit(solution)/shard_map/reduce_scatter | solution.py:54
  17.8 63.0 %collective-permute-start = (s32[2,256]{1,0:T(2,128)S(1)}, s32[2,256]{1,0:T(2,128)S(1)}, u32[]{:S(2)}, u32[]{:S(2)}) collective-permute-start(s32[2,256]{1,0:T(2,128)S(1)} %slice.152), channel_id=1, source_target_pairs={{0,32},{32,64},{64,96},{96,128},{128,160},{160,192},{192,224},{1,3... | collective-permute-start | bytes 6152 | tf_op jit(solution)/shard_map/ppermute | solution.py:46
  149.8 52.8 %copy-start.1 = (f32[64]{0:T(128)S(1)}, f32[64]{0:T(128)}, u32[]{:S(2)}) copy-start(f32[64]{0:T(128)} %param.9) | copy-start | bytes 772
  151.4 51.1 %reduce-scatter.5.cloned.1.call-start = ((), (), s32[]{:S(2)}) async-start(), calls=%async_computation.5 | async-start | bytes 1310720 | tf_op jit(solution)/shard_map/reduce_scatter | solution.py:54
  166.7 105.0 %all-gather.4.cloned.1.call-start = ((), (), s32[]{:S(2)}) async-start(), calls=%async_computation.6 | async-start | bytes 2359296 | tf_op jit(solution)/shard_map/all_gather | solution.py:70
  232.4 1.1 copy-start
  233.2 101.6 %all-gather.6.cloned.1.call-start = ((), (), s32[]{:S(2)}) async-start(), calls=%async_computation.7 | async-start | bytes 4718592 | tf_op jit(solution)/shard_map/all_gather | solution.py:70
Sparse Core Ops, SparseCore 0:
  151.6 15.0 reduce-scatter.2
  169.2 33.2 reduce-scatter.4
  233.3 38.2 all-gather.3
  273.3 54.4 all-gather.5
where the time goes:
time: 348 us; the launch traced here: 346 us
  other arithmetic  122 us (35%)
  waiting for transfers between devices  89.2 us (26%)
  matrix products  62.2 us (18%)
  blocking collectives  28.7 us (8%)
  local copies, waits for them, and re-layouts  17.3 us (5%)
  between operations  15.5 us (4%)
  starting transfers between devices  11.3 us (3%)
    dot_general x1, matrix products, on_device(): jnp.einsum('ij,bjc->bic', upper_part, current_rows, preferred_element_typ...  53.7 us
    convert_element_type x1, other arithmetic, on_device(): harmonic_design(phase[0], phase[1], orders, degrees, scales)  53.6 us
    reduce_scatter x2, waiting for transfers between devices, sum_in_order(): tiles = lax.psum_scatter(tiles, axes[k], scatter_dimension=0, tiled=True)  51 us
    all_gather x2, waiting for transfers between devices, picked(): lax.all_gather(x, axis)  37.9 us
    another operation x6, other arithmetic, on_device(): leading = jnp.linalg.cholesky(lead_rows)  33.9 us
    another operation x3, other arithmetic, on_device(): jax.scipy.linalg.solve_triangular(leading, spread.T, lower=True)  19.7 us
    all_to_all x1, blocking collectives, from_everyone(): lax.all_to_all(jnp.broadcast_to(x[None], (count, *x.shape)), axis, 0, 0,...  18.1 us
    all_gather x1, blocking collectives, picked(): lax.all_gather(x, axis)  10.6 us
  transfers between devices with their start and end apart: 6, of which 3 were waited for; matrix products, arithmetic and copies ran while one was open for 35% of the time, Pallas kernels for 0%

commit v1 on v0

v1 whole, which is shorter than its diff:
```python
import functools

import jax
import jax.numpy as jnp
from jax import lax
from jax.experimental import pallas as pl
from jax.experimental.pallas import tpu as pltpu
from jax.sharding import PartitionSpec as P

F32 = jnp.float32
BF16 = jnp.bfloat16
MESH = pl.DeviceIdType.MESH
HIGH = lax.Precision.HIGHEST
B = 256
BLK = 256
PERIOD = 4096
NX = 4
WAVE = (8.88573567404434, -58.45953046181323, 115.03267724691959, -100.39492606524867)
ROUND = 12582912.0
VMEM = pl.BlockSpec(memory_space=pltpu.VMEM)


def place():
    e, p, y = (lax.axis_index(a) for a in ("epoch", "prow", "pcol"))
    core, z_lo = e % 2, e // 2
    x, z_hi = p % NX, p // NX
    return x, y, z_hi * 4 + z_lo, core


def device(x, z, core):
    return {"epoch": (z % 4) * 2 + core, "prow": (z // 4) * NX + x}


def phase_kernel(steps_ref, phase_ref, every, send, recv):
    e = lax.axis_index("epoch")
    n = 8
    barrier = pltpu.get_barrier_semaphore()
    for i in range(1, n):
        pl.semaphore_signal(barrier, inc=1, device_id={"epoch": (e + i) % n}, device_id_type=MESH)
    pl.semaphore_wait(barrier, n - 1)
    copies = []
    for i in range(1, n):
        copy = pltpu.make_async_remote_copy(
            src_ref=steps_ref,
            dst_ref=every.at[e],
            send_sem=send.at[i],
            recv_sem=recv.at[i],
            device_id={"epoch": (e + i) % n},
            device_id_type=MESH,
        )
        copy.start()
        copies.append(copy)
    every[e] = steps_ref[...]
    tiles = steps_ref.shape[1]
    rows = n * 2 * tiles
    upper = (
        lax.broadcasted_iota(jnp.int32, (128, 128), 0)
        <= lax.broadcasted_iota(jnp.int32, (128, 128), 1)
    ).astype(BF16)
    r = lax.broadcasted_iota(jnp.int32, (rows, rows), 0)
    s = lax.broadcasted_iota(jnp.int32, (rows, rows), 1)
    same = (r // tiles) % 2 == (s // tiles) % 2
    key_r = (r // (2 * tiles)) * tiles + r % tiles
    key_s = (s // (2 * tiles)) * tiles + s % tiles
    before = jnp.where(same & (key_s < key_r), 1.0, 0.0).astype(F32)
    for copy in copies:
        copy.wait()
    x = every[...].reshape(rows, 128).astype(F32).astype(BF16)
    inside = jnp.dot(x, upper, preferred_element_type=F32)
    totals = jnp.broadcast_to(inside[:, 127:128], (rows, 128))
    earlier = jnp.dot(before, totals, precision=HIGH, preferred_element_type=F32)
    whole = (inside + earlier).astype(jnp.int32)
    phase_ref[...] = (whole & (PERIOD - 1)).astype(F32) * (1.0 / PERIOD)


def wave(turn, scale):
    turn = turn - 0.125
    whole = (turn + ROUND) - ROUND
    z = 0.25 - jnp.abs(turn - whole)
    s = z * z
    poly = WAVE[3]
    for c in (WAVE[2], WAVE[1], WAVE[0]):
        poly = poly * s + c
    return poly * (z * scale)


def tile_kernel(
    phase_ref, harm_ref, scale_ref, taps_ref, lead_ref, own_ref,
    colf, rowf, lowt, lowr, dcol, drow, fcol, frow,
):
    x, y, z, core = place()
    group = ((z % 4) * 2 + core) * 2 + z // 4
    blocks = (phase_ref.shape[0] // 4) // NX
    n_rows = rowf.shape[1]
    n_lead = n_rows - 256
    n_tiles = colf.shape[1]
    cols_here = n_tiles - 2

    def features(k):
        h = harm_ref[pl.ds(k, 1), :]
        return (
            lax.shift_right_logical(h, 6).astype(F32),
            (h & 63).astype(F32),
            scale_ref[pl.ds(k, 1), :],
        )

    def down(row):
        return jnp.transpose(jnp.broadcast_to(row, (128, 128)))

    for jt in range(n_tiles):
        k = jt if jt < 2 else y * cols_here + (jt - 2)
        for f, v in enumerate(features(k)):
            colf[f, jt] = v
    for half in range(2):
        for f, v in enumerate(features(group * 2 + half)):
            rowf[f, half * 128 : half * 128 + 128, :] = down(v)
    per = 128 // n_lead
    for f, v in enumerate(features(group // per)):
        lowr[...] = down(v)
        rowf[f, 256:, :] = lowr[pl.ds(pl.multiple_of((group % per) * n_lead, n_lead), n_lead), :]

    base = jnp.concatenate([taps_ref[0:1, :], taps_ref[1:2, :], jnp.zeros((1, 256), F32)], axis=1)
    full = pltpu.roll(
        jnp.broadcast_to(base, (512, 512)), 256, 1, stride=1, stride_axis=0
    )[:, :256]
    low_up = jnp.transpose(full).astype(BF16)
    lowt[...] = full.astype(BF16)

    @pl.loop(0, blocks + 1)
    def _(b):
        at = x * blocks + b - 1
        present = at >= 0
        at = jnp.maximum(at, 0)
        row0 = (at // 8) * 32 + (at % 8) * 2
        for half in range(2):
            q0 = phase_ref[pl.ds(row0 + half, 1), :]
            q1 = phase_ref[pl.ds(row0 + 16 + half, 1), :]
            q0d, q1d = down(q0), down(q1)
            where_t = pl.multiple_of(b * BLK + half * 128, 128)
            for jt in range(n_tiles):
                d = wave(q0d * colf[0, jt] + q1d * colf[1, jt], colf[2, jt])
                d = jnp.where(present, d, 0.0)
                dcol[pl.ds(where_t, 128), jt * 128 : jt * 128 + 128] = d.astype(BF16)
            for r0 in range(0, n_rows, 128):
                r1 = min(r0 + 128, n_rows)
                d = wave(q0 * rowf[0, r0:r1, :] + q1 * rowf[1, r0:r1, :], rowf[2, r0:r1, :])
                d = jnp.where(present, d, 0.0)
                drow[r0:r1, pl.ds(where_t, 128)] = d.astype(BF16)

    lowr2 = low_up

    @pl.loop(0, blocks)
    def _(b):
        t0 = pl.multiple_of(b * BLK, BLK)
        for j0 in range(0, n_tiles * 128, 256):
            f = jnp.dot(
                lowr2, dcol[pl.ds(t0, 2 * BLK), j0 : j0 + 256], preferred_element_type=F32
            )
            fcol[pl.ds(t0, BLK), j0 : j0 + 256] = f.astype(BF16)
        f = jnp.dot(drow[:, pl.ds(t0, 2 * BLK)], lowt[...], preferred_element_type=F32)
        frow[:, pl.ds(t0, BLK)] = f.astype(BF16)

    total = 1.0 / (blocks * BLK * NX)
    for j0 in range(0, n_tiles * 128, 256):
        g = jnp.dot(frow[...], fcol[:, j0 : j0 + 256], preferred_element_type=F32) * total
        own_ref[:, :, j0 : j0 + 256] = g[:256].reshape(NX, 64, 256)
        lead_ref[:, :, j0 : j0 + 256] = g[256:].reshape(NX, n_lead // NX, 256)


def exchange_kernel(
    lead_ref, own_ref, ridge_ref, mine_ref, slab_ref,
    slab, got_lead, got_own, send_lead, recv_lead, send_own, recv_own,
    send_z, recv_z, send_x, recv_x, send_c, recv_c,
):
    x, y, z, core = place()
    nz = 8
    width = lead_ref.shape[2]
    barrier = pltpu.get_barrier_semaphore()
    peers = [device((x + i) % NX, z, core) for i in range(1, NX)]
    tall = [device(x, (z + i) % nz, core) for i in range(1, nz)]
    other = device(x, z, 1 - core)
    for peer in peers + tall + [other]:
        pl.semaphore_signal(barrier, inc=1, device_id=peer, device_id_type=MESH)
    pl.semaphore_wait(barrier, len(peers) + len(tall) + 1)

    def put(src, dst, send, recv, peer):
        copy = pltpu.make_async_remote_copy(
            src_ref=src, dst_ref=dst, send_sem=send, recv_sem=recv,
            device_id=peer, device_id_type=MESH,
        )
        copy.start()
        return copy

    first = [
        put(lead_ref.at[(x + i) % NX], got_lead.at[i - 1], send_lead.at[i - 1], recv_lead.at[i - 1], peers[i - 1])
        for i in range(1, NX)
    ]
    owns = [
        put(own_ref.at[(x + i) % NX], got_own.at[i - 1], send_own.at[i - 1], recv_own.at[i - 1], peers[i - 1])
        for i in range(1, NX)
    ]
    for copy in first:
        copy.wait()
    slab[x, core, z, :, :width] = lead_ref[x] + got_lead[0] + got_lead[1] + got_lead[2]
    slab[x, core, z, :, width:] = jnp.broadcast_to(ridge_ref[...], (lead_ref.shape[1], 128))
    second = [
        put(slab.at[x, core, z], slab.at[x, core, z], send_z.at[i - 1], recv_z.at[i - 1], tall[i - 1])
        for i in range(1, nz)
    ]
    for copy in second:
        copy.wait()
    third = [
        put(slab.at[x, core], slab.at[x, core], send_x.at[i - 1], recv_x.at[i - 1], peers[i - 1])
        for i in range(1, NX)
    ]
    fourth = [put(slab.at[x, core], slab.at[x, core], send_c.at[0], recv_c.at[0], other)]
    for i in range(1, NX):
        third[i - 1].wait()
        xx = (x + NX - i) % NX
        fourth.append(put(slab.at[xx, core], slab.at[xx, core], send_c.at[i], recv_c.at[i], other))
    for copy in fourth:
        copy.wait()
    slab_ref[...] = slab[...]
    for copy in owns:
        copy.wait()
    mine_ref[...] = own_ref[x] + got_own[0] + got_own[1] + got_own[2]


def dot(a, b, dims=((1,), (0,))):
    return lax.dot_general(a, b, (dims, ((), ())), precision=HIGH, preferred_element_type=F32)


def inverse_factor(a):
    n = 128
    sub = lax.broadcasted_iota(jnp.int32, (8, 1), 0)
    lane = lax.broadcasted_iota(jnp.int32, (8, n), 1)
    row8 = lax.broadcasted_iota(jnp.int32, (8, n), 0)
    left = [a[8 * k : 8 * k + 8, :] for k in range(n // 8)]
    right = [jnp.where(lane == row8 + 8 * k, 1.0, 0.0).astype(F32) for k in range(n // 8)]
    for i in range(n):
        k, s = divmod(i, 8)
        top_l = left[k][s : s + 1, :]
        top_r = right[k][s : s + 1, :]
        inv = 1.0 / top_l[:, i : i + 1]
        for m in range(k, n // 8):
            ratio = left[m][:, i : i + 1] * inv
            if m == k:
                ratio = jnp.where(sub > s, ratio, 0.0)
            left[m] = left[m] - ratio * top_l
            right[m] = right[m] - ratio * top_r
    out = []
    for k in range(n // 8):
        diag = jnp.sum(jnp.where(lane == row8 + 8 * k, left[k], 0.0), axis=1, keepdims=True)
        out.append(right[k] * lax.rsqrt(diag))
    return jnp.concatenate(out, axis=0)


def finish_kernel(mine_ref, slab_ref, ridge_ref, panel_ref, schur_ref, full, winv):
    x, y, z, core = place()
    e, p = lax.axis_index("epoch"), lax.axis_index("prow")
    width = slab_ref.shape[4] - 128
    cols = width - B
    for xx in range(NX):
        for zz in range(8):
            for cc in range(2):
                g = ((zz % 4) * 2 + cc) * 2 + zz // 4
                r0 = 16 * g + 4 * xx
                full[r0 : r0 + 4, :] = slab_ref[xx, cc, zz, :, :width]
    lane = lax.broadcasted_iota(jnp.int32, (64, B), 1)
    sub = lax.broadcasted_iota(jnp.int32, (64, B), 0)
    for k in range(4):
        row = jnp.broadcast_to(slab_ref[k, 0, 0, 0:1, width:], (128, 128))
        ridge = jnp.transpose(row)[:64, 0:1]
        add = jnp.where(lane == sub + 64 * k, ridge, 0.0)
        full[64 * k : 64 * k + 64, 0:B] += add
        full[64 * k : 64 * k + 64, B : 2 * B] += jnp.where(y == 0, add, 0.0)
    w1 = inverse_factor(full[0:128, 0:128])
    low = full[128:256, 0:128]
    s = dot(low, w1, ((1,), (1,)))
    rest = full[128:256, 128:256] - dot(s, s, ((1,), (1,)))
    sw = dot(s, w1)
    w2 = inverse_factor(rest)
    winv[0:128, 0:128] = w1
    winv[0:128, 128:256] = jnp.zeros((128, 128), F32)
    winv[128:256, 0:128] = -dot(w2, sw)
    winv[128:256, 128:256] = w2
    first = (e * 8 + p) * 64
    own_ridge = jnp.transpose(jnp.broadcast_to(ridge_ref[...], (128, 128)))[:64, 0:1]
    lead = mine_ref[:, 0:B] + jnp.where(lane == sub + first, own_ridge, 0.0)
    panel = dot(lead, winv[...], ((1,), (1,)))
    panel_ref[...] = panel
    for j0 in range(0, cols, 256):
        right = dot(winv[...], full[:, B + j0 : B + j0 + 256])
        here = mine_ref[:, B + j0 : B + j0 + 256]
        here = here + jnp.where(lane + (y * cols + j0) == sub + first, own_ridge, 0.0)
        schur_ref[:, j0 : j0 + 256] = here - dot(panel, right)


def on_device(steps, harmonic, col_scale, taps, ridge):
    params = harmonic.shape[0]
    cols = params // 4
    width = cols + B
    steps3 = steps.reshape(2, 16, 128)
    phase = pl.pallas_call(
        phase_kernel,
        out_shape=jax.ShapeDtypeStruct((256, 128), F32),
        in_specs=[VMEM],
        out_specs=VMEM,
        scratch_shapes=[
            pltpu.VMEM((8, 2, 16, 128), jnp.int32),
            pltpu.SemaphoreType.DMA((8,)),
            pltpu.SemaphoreType.DMA((8,)),
        ],
        compiler_params=pltpu.CompilerParams(collective_id=0, has_side_effects=True),
        name="phases",
    )(steps3)
    here = 4096
    n_rows = 272
    lead, own = pl.pallas_call(
        tile_kernel,
        out_shape=(
            jax.ShapeDtypeStruct((NX, 4, width), F32),
            jax.ShapeDtypeStruct((NX, 64, width), F32),
        ),
        in_specs=[VMEM] * 4,
        out_specs=(VMEM, VMEM),
        scratch_shapes=[
            pltpu.VMEM((3, width // 128, 1, 128), F32),
            pltpu.VMEM((3, n_rows, 128), F32),
            pltpu.VMEM((512, 256), BF16),
            pltpu.VMEM((128, 128), F32),
            pltpu.VMEM((here + BLK, width), BF16),
            pltpu.VMEM((n_rows, here + BLK), BF16),
            pltpu.VMEM((here, width), BF16),
            pltpu.VMEM((n_rows, here), BF16),
        ],
        compiler_params=pltpu.CompilerParams(vmem_limit_bytes=60 * 1024 * 1024),
        name="tile",
    )(phase, harmonic.reshape(-1, 128), col_scale.reshape(-1, 128), taps.reshape(2, 128))
    ridge_row = jnp.pad(ridge.reshape(1, -1), ((0, 0), (0, 128 - ridge.shape[0])))
    dma = pltpu.SemaphoreType.DMA
    mine, slab = pl.pallas_call(
        exchange_kernel,
        out_shape=(
            jax.ShapeDtypeStruct((64, width), F32),
            jax.ShapeDtypeStruct((NX, 2, 8, 4, width + 128), F32),
        ),
        in_specs=[VMEM] * 3,
        out_specs=(VMEM, VMEM),
        scratch_shapes=[
            pltpu.VMEM((NX, 2, 8, 4, width + 128), F32),
            pltpu.VMEM((NX - 1, 4, width), F32),
            pltpu.VMEM((NX - 1, 64, width), F32),
            dma((3,)), dma((3,)), dma((3,)), dma((3,)),
            dma((7,)), dma((7,)), dma((3,)), dma((3,)), dma((4,)), dma((4,)),
        ],
        compiler_params=pltpu.CompilerParams(collective_id=1, has_side_effects=True),
        name="exchange",
    )(lead, own, ridge_row)
    return pl.pallas_call(
        finish_kernel,
        out_shape=(
            jax.ShapeDtypeStruct((64, B), F32),
            jax.ShapeDtypeStruct((64, cols), F32),
        ),
        in_specs=[VMEM] * 3,
        out_specs=(VMEM, VMEM),
        scratch_shapes=[pltpu.VMEM((B, width), F32), pltpu.VMEM((B, B), F32)],
        name="finish",
    )(mine, slab, ridge_row)


def solution(mesh):
    row = P(("epoch", "prow"))
    return jax.shard_map(
        on_device,
        mesh=mesh,
        in_specs=(P(None, "epoch"), P(), P(), P(), row),
        out_specs=(P(("epoch", "prow"), None), P(("epoch", "prow"), "pcol")),
        check_vma=False,
    )
```

time: 348 us -> 112 us (0.32)
  other arithmetic: 122 us -> 0 us
  Pallas kernels: 0 us -> 109 us
  waiting for transfers between devices: 89.2 us -> 0 us
  matrix products: 62.2 us -> 0 us
  blocking collectives: 28.7 us -> 0 us
  between operations: 15.5 us -> 0.65 us
  local copies, waits for them, and re-layouts: 17.3 us -> 2.57 us
  starting transfers between devices: 11.3 us -> 0 us
    pallas_call x0 -> x4, Pallas kernels: none -> 109 us  [the longest x1 35.6 us: on_device(): pl.pallas_call(exchange_kernel, out_shape=(jax.ShapeDtypeStruct((64, widt...]
    convert_element_type x2 -> x0, other arithmetic: 60.4 us -> none  [the longest x1 53.6 us: on_device(): harmonic_design(phase[0], phase[1], orders, degrees, scales)]
    dot_general x4 -> x0, matrix products: 59.3 us -> none  [the longest x1 53.7 us: on_device(): jnp.einsum('ij,bjc->bic', upper_part, current_rows, preferred_element_typ...]
    another operation x14 -> x0, other arithmetic: 55.3 us -> none  [the longest x6 33.9 us: on_device(): leading = jnp.linalg.cholesky(lead_rows)]
    reduce_scatter x2 -> x0, waiting for transfers between devices: 51 us -> none  [sum_in_order(): tiles = lax.psum_scatter(tiles, axes[k], scatter_dimension=0, tiled=True)]
    all_gather x2 -> x0, waiting for transfers between devices: 37.9 us -> none  [picked(): lax.all_gather(x, axis)]
    all_to_all x1 -> x0, blocking collectives: 18.1 us -> none  [from_everyone(): lax.all_to_all(jnp.broadcast_to(x[None], (count, *x.shape)), axis, 0, 0,...]
    all_gather x1 -> x0, blocking collectives: 10.6 us -> none  [picked(): lax.all_gather(x, axis)]
  transfers between devices with their start and end apart: 6 -> 0, of which waited for: 3 -> 0; matrix products, arithmetic and copies ran while one was open for 35% -> 0% of each run, Pallas kernels for 0% -> 0%
where the time goes in v1:
time: 112 us
  Pallas kernels  109 us (97%)
  local copies, waits for them, and re-layouts  2.57 us (2%)
    pallas_call x1, Pallas kernels, on_device(): pl.pallas_call(exchange_kernel, out_shape=(jax.ShapeDtypeStruct((64, widt...  35.6 us
    pallas_call x1, Pallas kernels, on_device(): pl.pallas_call(tile_kernel, out_shape=(jax.ShapeDtypeStruct((NX, 4, width...  34.5 us
    pallas_call x1, Pallas kernels, on_device(): pl.pallas_call(finish_kernel, out_shape=(jax.ShapeDtypeStruct((64, B), F3...  27.3 us
    pallas_call x1, Pallas kernels, on_device(): pl.pallas_call(phase_kernel, out_shape=jax.ShapeDtypeStruct((256, 128), F...  11.5 us

profile of v1, /device:TPU:1, one launch (start us, length us, event | category | flops | bytes accessed | tf_op | source)
XLA Modules:
  0.0 112.2 jit_solution(8194855936155732650)
XLA Ops:
  0.6 1.2 %pad.4.ridge_ref = f32[1,128]{1,0:T(1,128)} pad(f32[1,64]{1,0:T(1,128)} %bitcast.13, f32[]{:T(128)} %constant.2.clone.1), padding=0_0x0_64 | pad | bytes 772 | tf_op jit(solution)/shard_map/jit(_pad)/pad | solution.py:340
  1.9 1.3 %copy.9 = s32[1,2,16,128]{3,2,1,0:T(8,128)} copy(s32[1,2,16,128]{3,1,2,0:T(2,128)} %bitcast.11) | data formatting | bytes 32768
  3.2 11.5 %phases.1.phase_ref = f32[256,128]{1,0:T(8,128)} custom-call(s32[2,16,128]{2,1,0:T(8,128)} %bitcast.8), custom_call_target="tpu_custom_call" | custom-call | tf_op jit(solution)/shard_map/phases/pallas_call | solution.py:304
  14.8 34.5 %tile.1 = (f32[4,4,1280]{2,1,0:T(4,128)}, f32[4,64,1280]{2,1,0:T(8,128)}) custom-call(f32[256,128]{1,0:T(8,128)} %phases.1.phase_ref, s32[32,128]{1,0:T(8,128)} %bitcast.9, f32[32,128]{1,0:T(8,128)} %bitcast.10, f32[2,128]{1,0:T(2,128)} %bitcast.12), custom_call_target="tpu_custom_call" | custom-call | tf_op jit(solution)/shard_map/tile/pallas_call | solution.py:319
  49.3 35.6 %exchange.1 = (f32[64,1280]{1,0:T(8,128)}, f32[4,2,8,4,1408]{4,3,2,1,0:T(4,128)}) custom-call(f32[4,4,1280]{2,1,0:T(4,128)} %get-tuple-element.6.lead_ref, f32[4,64,1280]{2,1,0:T(8,128)} %get-tuple-element.7.own_ref, f32[1,128]{1,0:T(1,128)} %pad.4.ridge_ref), custom_call_target="tpu_custom_call" | custom-call | tf_op jit(solution)/shard_map/exchange/pallas_call | solution.py:342
  84.9 27.3 %finish.1 = (f32[64,256]{1,0:T(8,128)}, f32[64,1024]{1,0:T(8,128)}) custom-call(f32[64,1280]{1,0:T(8,128)} %get-tuple-element.8.mine_ref, f32[4,2,8,4,1408]{4,3,2,1,0:T(4,128)} %get-tuple-element.9.slab_ref, f32[1,128]{1,0:T(1,128)} %pad.4.ridge_ref), custom_call_target="tpu_custom_call" | custom-call | tf_op jit(solution)/shard_map/finish/pallas_call | solution.py:360

commit v2 on v1

v2 whole, which is shorter than its diff:
```python
import functools

import jax
import jax.numpy as jnp
from jax import lax
from jax.experimental import pallas as pl
from jax.experimental.pallas import tpu as pltpu
from jax.sharding import PartitionSpec as P

F32 = jnp.float32
BF16 = jnp.bfloat16
MESH = pl.DeviceIdType.MESH
HIGH = lax.Precision.HIGHEST
B = 256
BLK = 256
PERIOD = 4096
NX = 4
WAVE = (8.88573567404434, -58.45953046181323, 115.03267724691959, -100.39492606524867)
ROUND = 12582912.0
VMEM = pl.BlockSpec(memory_space=pltpu.VMEM)


def place():
    e, p, y = (lax.axis_index(a) for a in ("epoch", "prow", "pcol"))
    core, z_lo = e % 2, e // 2
    x, z_hi = p % NX, p // NX
    return x, y, z_hi * 4 + z_lo, core


def device(x, z, core):
    return {"epoch": (z % 4) * 2 + core, "prow": (z // 4) * NX + x}


def phase_kernel(steps_ref, ridge_ref, phase_ref, ridge0_ref, every, every_ridge, send, recv, send_r, recv_r):
    e = lax.axis_index("epoch")
    n = 8
    barrier = pltpu.get_barrier_semaphore()
    for i in range(1, n):
        pl.semaphore_signal(barrier, inc=1, device_id={"epoch": (e + i) % n}, device_id_type=MESH)
    pl.semaphore_wait(barrier, n - 1)
    copies = []
    for i in range(1, n):
        copy = pltpu.make_async_remote_copy(
            src_ref=steps_ref,
            dst_ref=every.at[e],
            send_sem=send.at[i],
            recv_sem=recv.at[i],
            device_id={"epoch": (e + i) % n},
            device_id_type=MESH,
        )
        copy.start()
        copies.append(copy)
        copy = pltpu.make_async_remote_copy(
            src_ref=ridge_ref,
            dst_ref=every_ridge.at[e],
            send_sem=send_r.at[i],
            recv_sem=recv_r.at[i],
            device_id={"epoch": (e + i) % n},
            device_id_type=MESH,
        )
        copy.start()
        copies.append(copy)
    every[e] = steps_ref[...]
    every_ridge[e] = ridge_ref[...]
    tiles = steps_ref.shape[1]
    rows = n * 2 * tiles
    upper = (
        lax.broadcasted_iota(jnp.int32, (128, 128), 0)
        <= lax.broadcasted_iota(jnp.int32, (128, 128), 1)
    ).astype(BF16)
    r = lax.broadcasted_iota(jnp.int32, (rows, rows), 0)
    s = lax.broadcasted_iota(jnp.int32, (rows, rows), 1)
    same = (r // tiles) % 2 == (s // tiles) % 2
    key_r = (r // (2 * tiles)) * tiles + r % tiles
    key_s = (s // (2 * tiles)) * tiles + s % tiles
    before = jnp.where(same & (key_s < key_r), 1.0, 0.0).astype(F32)
    for copy in copies:
        copy.wait()
    x = every[...].reshape(rows, 128).astype(F32).astype(BF16)
    inside = jnp.dot(x, upper, preferred_element_type=F32)
    totals = jnp.broadcast_to(inside[:, 127:128], (rows, 128))
    earlier = jnp.dot(before, totals, precision=HIGH, preferred_element_type=F32)
    ridge0_ref[...] = every_ridge[0]
    whole = (inside + earlier).astype(jnp.int32)
    phase_ref[...] = (whole & (PERIOD - 1)).astype(F32) * (1.0 / PERIOD)


def wave(turn, scale):
    turn = turn - 0.125
    whole = (turn + ROUND) - ROUND
    z = 0.25 - jnp.abs(turn - whole)
    s = z * z
    poly = WAVE[3]
    for c in (WAVE[2], WAVE[1], WAVE[0]):
        poly = poly * s + c
    return poly * (z * scale)


def tile_kernel(
    phase_ref, harm_ref, scale_ref, taps_ref,
    la_ref, lb_ref, oa_ref, ob_ref, oc_ref,
    colf, rowf, lowt, lowr, dcol, drow, fcol, frow, held,
):
    x, y, z, core = place()
    group = ((z % 4) * 2 + core) * 2 + z // 4
    blocks = (phase_ref.shape[0] // 4) // NX
    n_rows = rowf.shape[1]
    n_lead = n_rows - 256
    n_tiles = colf.shape[1]
    cols_here = n_tiles - 2

    def features(k):
        h = harm_ref[pl.ds(k, 1), :]
        return (
            lax.shift_right_logical(h, 6).astype(F32),
            (h & 63).astype(F32),
            scale_ref[pl.ds(k, 1), :],
        )

    def down(row):
        return jnp.transpose(jnp.broadcast_to(row, (128, 128)))

    for jt in range(n_tiles):
        k = jt if jt < 2 else y * cols_here + (jt - 2)
        for f, v in enumerate(features(k)):
            colf[f, jt] = v
    for half in range(2):
        for f, v in enumerate(features(group * 2 + half)):
            rowf[f, half * 128 : half * 128 + 128, :] = down(v)
    per = 128 // n_lead
    for f, v in enumerate(features(group // per)):
        lowr[...] = down(v)
        rowf[f, 256:, :] = lowr[pl.ds(pl.multiple_of((group % per) * n_lead, n_lead), n_lead), :]

    base = jnp.concatenate([taps_ref[0:1, :], taps_ref[1:2, :], jnp.zeros((1, 256), F32)], axis=1)
    full = pltpu.roll(
        jnp.broadcast_to(base, (512, 512)), 256, 1, stride=1, stride_axis=0
    )[:, :256]
    low_up = jnp.transpose(full).astype(BF16)
    lowt[...] = full.astype(BF16)

    @pl.loop(0, blocks + 1)
    def _(b):
        at = x * blocks + b - 1
        present = at >= 0
        at = jnp.maximum(at, 0)
        row0 = (at // 8) * 32 + (at % 8) * 2
        for half in range(2):
            q0 = phase_ref[pl.ds(row0 + half, 1), :]
            q1 = phase_ref[pl.ds(row0 + 16 + half, 1), :]
            q0d, q1d = down(q0), down(q1)
            where_t = pl.multiple_of(b * BLK + half * 128, 128)
            for jt in range(n_tiles):
                d = wave(q0d * colf[0, jt] + q1d * colf[1, jt], colf[2, jt])
                d = jnp.where(present, d, 0.0)
                dcol[pl.ds(where_t, 128), jt * 128 : jt * 128 + 128] = d.astype(BF16)
            for r0 in range(0, n_rows, 128):
                r1 = min(r0 + 128, n_rows)
                d = wave(q0 * rowf[0, r0:r1, :] + q1 * rowf[1, r0:r1, :], rowf[2, r0:r1, :])
                d = jnp.where(present, d, 0.0)
                drow[r0:r1, pl.ds(where_t, 128)] = d.astype(BF16)

    lowr2 = low_up

    @pl.loop(0, blocks)
    def _(b):
        t0 = pl.multiple_of(b * BLK, BLK)
        for j0 in range(0, n_tiles * 128, 256):
            f = jnp.dot(
                lowr2, dcol[pl.ds(t0, 2 * BLK), j0 : j0 + 256], preferred_element_type=F32
            )
            fcol[pl.ds(t0, BLK), j0 : j0 + 256] = f.astype(BF16)
        f = jnp.dot(drow[:, pl.ds(t0, 2 * BLK)], lowt[...], preferred_element_type=F32)
        frow[:, pl.ds(t0, BLK)] = f.astype(BF16)

    total = 1.0 / (blocks * BLK * NX)
    for j0 in range(0, n_tiles * 128, 256):
        g = jnp.dot(frow[...], fcol[:, j0 : j0 + 256], preferred_element_type=F32) * total
        if j0 == 0:
            oa_ref[...] = g[:256].reshape(NX, 64, 256)
            la_ref[...] = g[256:]
        else:
            held[...] = g[:256]
            ob_ref[:, :, j0 - 256 : j0] = g[:256].astype(BF16).reshape(NX, 64, 256)
            oc_ref[:, j0 - 256 : j0] = held[pl.ds(pl.multiple_of(x * 64, 64), 64), :]
            lb_ref[:, j0 - 256 : j0] = g[256:]


def dot(a, b, dims=((1,), (0,))):
    return lax.dot_general(a, b, (dims, ((), ())), precision=HIGH, preferred_element_type=F32)


def split3(v):
    hi = v.astype(BF16)
    v = v - hi.astype(F32)
    mid = v.astype(BF16)
    low = (v - mid.astype(F32)).astype(BF16)
    return hi, mid, low


NB = 32


def block_inverse(a):
    sub = lax.broadcasted_iota(jnp.int32, (NB, 1), 0)
    lane = lax.broadcasted_iota(jnp.int32, (NB, NB), 1)
    row = lax.broadcasted_iota(jnp.int32, (NB, NB), 0)
    eye = jnp.where(lane == row, 1.0, 0.0).astype(F32)
    m = jnp.concatenate([a, eye, jnp.zeros((NB, 128 - 2 * NB), F32)], axis=1)
    for i in range(NB):
        top = m[i : i + 1, :]
        scaled = top * (1.0 / top[:, i : i + 1])
        m = m - jnp.where(sub > i, m[:, i : i + 1], 0.0) * scaled
    diag = jnp.sum(m[:, :NB] * eye, axis=1, keepdims=True)
    return m[:, NB : 2 * NB] * lax.rsqrt(diag)


def final_kernel(
    la_ref, lb_ref, oa_ref, ob_ref, oc_ref, ridge0_ref, ridge_ref, panel_ref, schur_ref,
    slab_a, slab_b, got_la, got_lb, got_oa, got_ob, ridge4, ridge_far, mat,
    s_la, r_la, s_lb, r_lb, s_oa, r_oa, s_ob, r_ob, s_r, r_r, s_f, r_f,
    s_za, r_za, s_zb, r_zb, s_ca, r_ca, s_cb, r_cb,
):
    x, y, z, core = place()
    e, p = lax.axis_index("epoch"), lax.axis_index("prow")
    nz = 8

    def group(zz, cc):
        return ((zz % 4) * 2 + cc) * 2 + zz // 4

    g = group(z, core)
    barrier = pltpu.get_barrier_semaphore()
    peers = [device((x + i) % NX, z, core) for i in range(1, NX)]
    tall = [device(x, (z + i) % nz, core) for i in range(1, nz)]
    other = device(x, z, 1 - core)
    for peer in peers + tall + [other]:
        pl.semaphore_signal(barrier, inc=1, device_id=peer, device_id_type=MESH)
    pl.semaphore_wait(barrier, len(peers) + len(tall) + 1)

    def put(src, dst, send, recv, peer):
        copy = pltpu.make_async_remote_copy(
            src_ref=src, dst_ref=dst, send_sem=send, recv_sem=recv,
            device_id=peer, device_id_type=MESH,
        )
        copy.start()
        return copy

    def to_x(src, got, send, recv):
        return [put(src(i), got.at[i - 1], send.at[i - 1], recv.at[i - 1], peers[i - 1]) for i in range(1, NX)]

    def to_z(slab, send, recv):
        return [put(slab.at[g], slab.at[g], send.at[i - 1], recv.at[i - 1], tall[i - 1]) for i in range(1, nz)]

    def to_core(slab, send, recv, i):
        k = group((z + nz - i) % nz, core)
        return put(slab.at[k], slab.at[k], send.at[i], recv.at[i], other)

    lead_a = to_x(lambda i: la_ref, got_la, s_la, r_la)
    ridges = [
        put(ridge0_ref, ridge4.at[x], s_r.at[i - 1], r_r.at[i - 1], peers[i - 1])
        for i in range(1, NX)
    ]
    lead_b = to_x(lambda i: lb_ref, got_lb, s_lb, r_lb)
    ridge4[x] = ridge0_ref[...]
    for copy in lead_a:
        copy.wait()
    slab_a[g] = la_ref[...] + got_la[0] + got_la[1] + got_la[2]
    z_a = to_z(slab_a, s_za, r_za)
    c_a = [to_core(slab_a, s_ca, r_ca, 0)]
    for copy in ridges:
        copy.wait()
    far = put(ridge4, ridge_far, s_f, r_f, device(x, (z + 4) % nz, core))
    for copy in lead_b:
        copy.wait()
    slab_b[g] = lb_ref[...] + got_lb[0] + got_lb[1] + got_lb[2]
    z_b = to_z(slab_b, s_zb, r_zb)
    c_b = [to_core(slab_b, s_cb, r_cb, 0)]
    own_a = to_x(lambda i: oa_ref.at[(x + i) % NX], got_oa, s_oa, r_oa)
    own_b = to_x(lambda i: ob_ref.at[(x + i) % NX], got_ob, s_ob, r_ob)
    for i in range(1, nz):
        z_a[i - 1].wait()
        c_a.append(to_core(slab_a, s_ca, r_ca, i))
    far.wait()
    for copy in c_a:
        copy.wait()

    lane = lax.broadcasted_iota(jnp.int32, (64, B), 1)
    sub = lax.broadcasted_iota(jnp.int32, (64, B), 0)

    def column(row):
        return jnp.transpose(jnp.broadcast_to(row, (128, 128)))[:64, 0:1]

    lead_ridge = [column(jnp.where(z < 4, ridge4[k], ridge_far[k])) for k in range(4)]
    for k in range(4):
        rows = slab_a[4 * k : 4 * k + 4].reshape(64, B)
        mat[64 * k : 64 * k + 64, 0:B] = rows + jnp.where(lane == sub + 64 * k, lead_ridge[k], 0.0)
        mat[64 * k : 64 * k + 64, B:] = jnp.where(lane == sub + 64 * k, 1.0, 0.0).astype(F32)

    nxt = mat[0:NB, 0:NB]
    for j in range(B // NB):
        if j == B // NB // 2:
            for i in range(1, nz):
                z_b[i - 1].wait()
                c_b.append(to_core(slab_b, s_cb, r_cb, i))
        r0, r1 = NB * j, NB * j + NB
        w = block_inverse(nxt)
        rj = dot(w, mat[r0:r1, :])
        mat[r0:r1, :] = rj
        if r1 < B:
            hi, mid, low = split3(rj)
            left = jnp.concatenate([hi, hi, mid, hi, low, mid], axis=0)
            right = jnp.concatenate([hi, mid, hi, low, hi, mid], axis=0)
            dims = (((0,), (0,)), ((), ()))
            c0 = (r1 // 128) * 128
            at = lax.dot_general(left[:, c0:B], right[:, c0:B], dims, preferred_element_type=F32)
            nxt = mat[r1 : r1 + NB, r1 : r1 + NB] - at[r1 - c0 : r1 - c0 + NB, r1 - c0 : r1 - c0 + NB]
            mat[r1:B, c0:B] -= at[r1 - c0 :, :]
            w1 = B + ((r1 + 127) // 128) * 128
            aw = lax.dot_general(left[:, c0:B], right[:, B:w1], dims, preferred_element_type=F32)
            mat[r1:B, B:w1] -= aw[r1 - c0 :, :]

    for copy in own_a:
        copy.wait()
    first = (e * 8 + p) * 64
    own_ridge = column(ridge_ref[...])
    winv = mat[:, B:]
    lead = oa_ref[x] + got_oa[0] + got_oa[1] + got_oa[2]
    lead = lead + jnp.where(lane == sub + first, own_ridge, 0.0)
    panel = dot(lead, winv, ((1,), (1,)))
    panel_ref[...] = panel
    for copy in c_b:
        copy.wait()
    for copy in own_b:
        copy.wait()
    cols = lb_ref.shape[1]
    for j0 in range(0, cols, B):
        here = slab_b[:, :, j0 : j0 + B].reshape(B, B)
        if j0 == 0:
            add = [jnp.where((lane == sub + 64 * k) & (y == 0), lead_ridge[k], 0.0) for k in range(4)]
            here = here + jnp.concatenate(add, axis=0)
        right = dot(winv, here)
        at = slice(j0, j0 + B)
        tile = oc_ref[:, at] + got_ob[0, :, at].astype(F32)
        tile = tile + got_ob[1, :, at].astype(F32) + got_ob[2, :, at].astype(F32)
        tile = tile + jnp.where(lane + (y * cols + j0) == sub + first, own_ridge, 0.0)
        schur_ref[:, at] = tile - dot(panel, right)


def on_device(steps, harmonic, col_scale, taps, ridge):
    params = harmonic.shape[0]
    cols = params // 4
    width = cols + B
    dma = pltpu.SemaphoreType.DMA
    steps3 = steps.reshape(2, 16, 128)
    ridge_row = jnp.pad(ridge.reshape(1, -1), ((0, 0), (0, 128 - ridge.shape[0])))
    phase, ridge0 = pl.pallas_call(
        phase_kernel,
        out_shape=(
            jax.ShapeDtypeStruct((256, 128), F32),
            jax.ShapeDtypeStruct((1, 128), F32),
        ),
        in_specs=[VMEM] * 2,
        out_specs=(VMEM, VMEM),
        scratch_shapes=[
            pltpu.VMEM((8, 2, 16, 128), jnp.int32),
            pltpu.VMEM((8, 1, 128), F32),
            dma((8,)), dma((8,)), dma((8,)), dma((8,)),
        ],
        compiler_params=pltpu.CompilerParams(collective_id=0, has_side_effects=True),
        name="phases",
    )(steps3, ridge_row)
    here = 4096
    n_rows = 272
    parts = pl.pallas_call(
        tile_kernel,
        out_shape=(
            jax.ShapeDtypeStruct((16, B), F32),
            jax.ShapeDtypeStruct((16, cols), F32),
            jax.ShapeDtypeStruct((NX, 64, B), F32),
            jax.ShapeDtypeStruct((NX, 64, cols), BF16),
            jax.ShapeDtypeStruct((64, cols), F32),
        ),
        in_specs=[VMEM] * 4,
        out_specs=(VMEM,) * 5,
        scratch_shapes=[
            pltpu.VMEM((3, width // 128, 1, 128), F32),
            pltpu.VMEM((3, n_rows, 128), F32),
            pltpu.VMEM((512, 256), BF16),
            pltpu.VMEM((128, 128), F32),
            pltpu.VMEM((here + BLK, width), BF16),
            pltpu.VMEM((n_rows, here + BLK), BF16),
            pltpu.VMEM((here, width), BF16),
            pltpu.VMEM((n_rows, here), BF16),
            pltpu.VMEM((256, 256), F32),
        ],
        compiler_params=pltpu.CompilerParams(vmem_limit_bytes=60 * 1024 * 1024),
        name="tile",
    )(phase, harmonic.reshape(-1, 128), col_scale.reshape(-1, 128), taps.reshape(2, 128))
    return pl.pallas_call(
        final_kernel,
        out_shape=(
            jax.ShapeDtypeStruct((64, B), F32),
            jax.ShapeDtypeStruct((64, cols), F32),
        ),
        in_specs=[VMEM] * 7,
        out_specs=(VMEM, VMEM),
        scratch_shapes=[
            pltpu.VMEM((16, 16, B), F32),
            pltpu.VMEM((16, 16, cols), F32),
            pltpu.VMEM((NX - 1, 16, B), F32),
            pltpu.VMEM((NX - 1, 16, cols), F32),
            pltpu.VMEM((NX - 1, 64, B), F32),
            pltpu.VMEM((NX - 1, 64, cols), BF16),
            pltpu.VMEM((NX, 1, 128), F32),
            pltpu.VMEM((NX, 1, 128), F32),
            pltpu.VMEM((B, 2 * B), F32),
            *([dma((3,))] * 10), dma, dma, *([dma((7,))] * 4), *([dma((8,))] * 4),
        ],
        compiler_params=pltpu.CompilerParams(collective_id=1, has_side_effects=True),
        name="final",
    )(*parts, ridge0, ridge_row)


def solution(mesh):
    row = P(("epoch", "prow"))
    return jax.shard_map(
        on_device,
        mesh=mesh,
        in_specs=(P(None, "epoch"), P(), P(), P(), row),
        out_specs=(P(("epoch", "prow"), None), P(("epoch", "prow"), "pcol")),
        check_vma=False,
    )
```

time: 112 us -> 102 us (0.911)
  Pallas kernels: 109 us -> 95.5 us
  local copies, waits for them, and re-layouts: 2.57 us -> 5.65 us
    pallas_call x4 -> x3, Pallas kernels: 109 us -> 95.5 us  [the longest x1 49.4 us: on_device(): pl.pallas_call(final_kernel, out_shape=(jax.ShapeDtypeStruct((64, B), F32...]
    unnamed x1 -> x5, local copies, waits for them, and re-layouts: 1.32 us -> 5.12 us
where the time goes in v2:
time: 102 us
  Pallas kernels  95.5 us (94%)
  local copies, waits for them, and re-layouts  5.65 us (6%)
    pallas_call x1, Pallas kernels, on_device(): pl.pallas_call(final_kernel, out_shape=(jax.ShapeDtypeStruct((64, B), F32...  49.4 us
    pallas_call x1, Pallas kernels, on_device(): pl.pallas_call(tile_kernel, out_shape=(jax.ShapeDtypeStruct((16, B), F32)...  34.3 us
    pallas_call x1, Pallas kernels, on_device(): pl.pallas_call(phase_kernel, out_shape=(jax.ShapeDtypeStruct((256, 128),...  11.9 us
    unnamed x5, local copies, waits for them, and re-layouts  5.12 us

profile of v2, /device:TPU:1, one launch (start us, length us, event | category | flops | bytes accessed | tf_op | source)
XLA Modules:
  0.0 101.8 jit_solution(8120567237089414718)
XLA Ops:
  0.6 0.0 copy-start
  0.6 0.6 copy-done
  1.3 0.5 pad.4.ridge_ref
  1.8 1.3 %copy.9 = s32[1,2,16,128]{3,2,1,0:T(8,128)} copy(s32[1,2,16,128]{3,1,2,0:T(2,128)} %bitcast.11) | data formatting | bytes 32768
  3.1 11.9 %phases.1 = (f32[256,128]{1,0:T(8,128)}, f32[1,128]{1,0:T(1,128)}) custom-call(s32[2,16,128]{2,1,0:T(8,128)} %bitcast.8, f32[1,128]{1,0:T(1,128)} %pad.4.ridge_ref), custom_call_target="tpu_custom_call" | custom-call | tf_op jit(solution)/shard_map/phases/pallas_call | solution.py:356
  15.0 34.3 %tile.1 = (f32[16,256]{1,0:T(8,128)}, f32[16,1024]{1,0:T(8,128)}, f32[4,64,256]{2,1,0:T(8,128)}, bf16[4,64,1024]{2,1,0:T(8,128)(2,1)}, f32[64,1024]{1,0:T(8,128)}) custom-call(f32[256,128]{1,0:T(8,128)} %get-tuple-element.9.phase_ref, s32[32,128]{1,0:T(8,128)} %bitcast.9, f32[32,128]{1,0:T(8,128)} %bitcast.10, f32[2,128]{1,0:T(2,128)} %bitcast.12), custom_call_target="tpu_custom_call" | custom-call | tf_op jit(solution)/shard_map/tile/pallas_call | solution.py:374
  49.3 49.4 %final.1 = (f32[64,256]{1,0:T(8,128)}, f32[64,1024]{1,0:T(8,128)}) custom-call(f32[16,256]{1,0:T(8,128)} %get-tuple-element.10.la_ref, f32[16,1024]{1,0:T(8,128)} %get-tuple-element.11.lb_ref, f32[4,64,256]{2,1,0:T(8,128)} %get-tuple-element.12.oa_ref, bf16[4,64,1024]{2,1,0:T(8,128)(2,1)} %get-tuple-element.13.ob_ref, f32[64,1024]{1,0:T(8,128)} %get-tuple-element.14.oc_ref, ...), custom_call_target="tpu_custom_call" | custom-call | tf_op jit(solution)/shard_map/final/pallas_call | solution.py:399
  98.6 1.5 %copy.12 = f32[64,256]{1,0:T(8,128)} copy(f32[64,256]{1,0:T(8,128)} %get-tuple-element.18) | data formatting | bytes 131072
  100.1 1.7 %copy.13 = f32[64,1024]{1,0:T(8,128)} copy(f32[64,1024]{1,0:T(8,128)} %get-tuple-element.19) | data formatting | bytes 524288
Async XLA Ops:
  0.6 0.7 copy-start

commit v3 on v2

--- a/solution.py
+++ b/solution.py
@@ -86,7 +86,6 @@
 
 
 def wave(turn, scale):
-    turn = turn - 0.125
     whole = (turn + ROUND) - ROUND
     z = 0.25 - jnp.abs(turn - whole)
     s = z * z
@@ -96,85 +95,127 @@
     return poly * (z * scale)
 
 
+def halves(v):
+    hi = jnp.floor(v * 64.0) * (1.0 / 64.0)
+    return hi, v - hi
+
+
 def tile_kernel(
     phase_ref, harm_ref, scale_ref, taps_ref,
     la_ref, lb_ref, oa_ref, ob_ref, oc_ref,
-    colf, rowf, lowt, lowr, dcol, drow, fcol, frow, held,
+    colf, cols_s, rowf, rows_s, lowt, lowr, d0, d1, d2, e0, e1, e2, fcol, frow, held,
 ):
     x, y, z, core = place()
     group = ((z % 4) * 2 + core) * 2 + z // 4
     blocks = (phase_ref.shape[0] // 4) // NX
-    n_rows = rowf.shape[1]
+    n_rows = rows_s.shape[0]
     n_lead = n_rows - 256
-    n_tiles = colf.shape[1]
+    n_tiles = colf.shape[1] // 128
     cols_here = n_tiles - 2
+    dcol, drow = (d0, d1, d2), (e0, e1, e2)
 
     def features(k):
         h = harm_ref[pl.ds(k, 1), :]
-        return (
-            lax.shift_right_logical(h, 6).astype(F32),
-            (h & 63).astype(F32),
-            scale_ref[pl.ds(k, 1), :],
+        order = lax.shift_right_logical(h, 6).astype(F32)
+        degree = (h & 63).astype(F32)
+        shift = jnp.full((1, 128), -0.125, F32)
+        rows = jnp.concatenate(
+            [order, order, degree, degree, shift, jnp.zeros((11, 128), F32)], axis=0
         )
+        return rows, scale_ref[pl.ds(k, 1), :]
 
     def down(row):
         return jnp.transpose(jnp.broadcast_to(row, (128, 128)))
 
     for jt in range(n_tiles):
         k = jt if jt < 2 else y * cols_here + (jt - 2)
-        for f, v in enumerate(features(k)):
-            colf[f, jt] = v
+        rows, scale = features(k)
+        colf[:, jt * 128 : jt * 128 + 128] = rows.astype(BF16)
+        cols_s[:, jt * 128 : jt * 128 + 128] = scale
     for half in range(2):
-        for f, v in enumerate(features(group * 2 + half)):
-            rowf[f, half * 128 : half * 128 + 128, :] = down(v)
+        rows, scale = features(group * 2 + half)
+        rowf[half * 128 : half * 128 + 128, :] = jnp.transpose(rows).astype(BF16)
+        rows_s[half * 128 : half * 128 + 128, :] = down(scale)
     per = 128 // n_lead
-    for f, v in enumerate(features(group // per)):
-        lowr[...] = down(v)
-        rowf[f, 256:, :] = lowr[pl.ds(pl.multiple_of((group % per) * n_lead, n_lead), n_lead), :]
+    rows, scale = features(group // per)
+    piece = pl.ds(pl.multiple_of((group % per) * n_lead, n_lead), n_lead)
+    lowr[...] = down(scale)
+    rows_s[256:, :] = lowr[piece, :]
+    lowr[:, 0:16] = jnp.transpose(rows)
+    rowf[256:, :] = lowr[piece, 0:16].astype(BF16)
 
     base = jnp.concatenate([taps_ref[0:1, :], taps_ref[1:2, :], jnp.zeros((1, 256), F32)], axis=1)
     full = pltpu.roll(
         jnp.broadcast_to(base, (512, 512)), 256, 1, stride=1, stride_axis=0
     )[:, :256]
+    lowt[...] = full.astype(BF16)
     low_up = jnp.transpose(full).astype(BF16)
-    lowt[...] = full.astype(BF16)
-
-    @pl.loop(0, blocks + 1)
-    def _(b):
-        at = x * blocks + b - 1
-        present = at >= 0
-        at = jnp.maximum(at, 0)
+
+    def phases_of(b):
+        at = jnp.maximum(x * blocks + b - 1, 0)
         row0 = (at // 8) * 32 + (at % 8) * 2
-        for half in range(2):
-            q0 = phase_ref[pl.ds(row0 + half, 1), :]
-            q1 = phase_ref[pl.ds(row0 + 16 + half, 1), :]
-            q0d, q1d = down(q0), down(q1)
-            where_t = pl.multiple_of(b * BLK + half * 128, 128)
-            for jt in range(n_tiles):
-                d = wave(q0d * colf[0, jt] + q1d * colf[1, jt], colf[2, jt])
-                d = jnp.where(present, d, 0.0)
-                dcol[pl.ds(where_t, 128), jt * 128 : jt * 128 + 128] = d.astype(BF16)
-            for r0 in range(0, n_rows, 128):
-                r1 = min(r0 + 128, n_rows)
-                d = wave(q0 * rowf[0, r0:r1, :] + q1 * rowf[1, r0:r1, :], rowf[2, r0:r1, :])
-                d = jnp.where(present, d, 0.0)
-                drow[r0:r1, pl.ds(where_t, 128)] = d.astype(BF16)
-
-    lowr2 = low_up
-
-    @pl.loop(0, blocks)
-    def _(b):
-        t0 = pl.multiple_of(b * BLK, BLK)
-        for j0 in range(0, n_tiles * 128, 256):
-            f = jnp.dot(
-                lowr2, dcol[pl.ds(t0, 2 * BLK), j0 : j0 + 256], preferred_element_type=F32
+        parts = []
+        for a in range(2):
+            q = jnp.concatenate(
+                [phase_ref[pl.ds(row0 + 16 * a + half, 1), :] for half in range(2)], axis=1
             )
-            fcol[pl.ds(t0, BLK), j0 : j0 + 256] = f.astype(BF16)
-        f = jnp.dot(drow[:, pl.ds(t0, 2 * BLK)], lowt[...], preferred_element_type=F32)
-        frow[:, pl.ds(t0, BLK)] = f.astype(BF16)
+            parts += list(halves(q))
+        parts += [jnp.ones((1, BLK), F32), jnp.zeros((11, BLK), F32)]
+        return jnp.concatenate(parts, axis=0).astype(BF16)
+
+    def design(qf, slot, j0):
+        turn = lax.dot_general(
+            qf, colf[:, j0 : j0 + 256], (((0,), (0,)), ((), ())), preferred_element_type=F32
+        )
+        d = wave(turn, cols_s[:, j0 : j0 + 256])
+        dcol[slot][:, j0 : j0 + 256] = d.astype(BF16)
+
+    def design_rows(qf, slot):
+        turn = jnp.dot(rowf[...], qf, preferred_element_type=F32)
+        scale = rows_s[...]
+        d = wave(turn, jnp.concatenate([scale, scale], axis=1))
+        drow[slot][...] = d.astype(BF16)
+
+    def filter_cols(b, s0, s1, j0):
+        f = jnp.dot(low_up[:, :BLK], dcol[s0][:, j0 : j0 + 256], preferred_element_type=F32)
+        f = f + jnp.dot(low_up[:, BLK:], dcol[s1][:, j0 : j0 + 256], preferred_element_type=F32)
+        fcol[pl.ds(pl.multiple_of(b * BLK, BLK), BLK), j0 : j0 + 256] = f.astype(BF16)
+
+    def filter_rows(b, s0, s1):
+        f = jnp.dot(drow[s0][...], lowt[:BLK, :], preferred_element_type=F32)
+        f = f + jnp.dot(drow[s1][...], lowt[BLK:, :], preferred_element_type=F32)
+        frow[:, pl.ds(pl.multiple_of(b * BLK, BLK), BLK)] = f.astype(BF16)
+
+    wide = range(0, n_tiles * 128, 256)
+    for b in range(2):
+        qf = phases_of(b)
+        for j0 in wide:
+            design(qf, b, j0)
+        design_rows(qf, b)
+
+    @pl.when(x == 0)
+    def _():
+        d0[...] = jnp.zeros_like(d0)
+        e0[...] = jnp.zeros_like(e0)
+
+    @pl.loop(0, blocks // 3)
+    def _(step):
+        for s in range(3):
+            b = step * 3 + s
+            qf = phases_of(b + 2)
+            for j0 in wide:
+                filter_cols(b, s, (s + 1) % 3, j0)
+                design(qf, (s + 2) % 3, j0)
+            filter_rows(b, s, (s + 1) % 3)
+            design_rows(qf, (s + 2) % 3)
+
+    for b in range(blocks // 3 * 3, blocks):
+        for j0 in wide:
+            filter_cols(b, b % 3, (b + 1) % 3, j0)
+        filter_rows(b, b % 3, (b + 1) % 3)
 
     total = 1.0 / (blocks * BLK * NX)
-    for j0 in range(0, n_tiles * 128, 256):
+    for j0 in wide:
         g = jnp.dot(frow[...], fcol[:, j0 : j0 + 256], preferred_element_type=F32) * total
         if j0 == 0:
             oa_ref[...] = g[:256].reshape(NX, 64, 256)
@@ -383,12 +424,14 @@
         in_specs=[VMEM] * 4,
         out_specs=(VMEM,) * 5,
         scratch_shapes=[
-            pltpu.VMEM((3, width // 128, 1, 128), F32),
-            pltpu.VMEM((3, n_rows, 128), F32),
+            pltpu.VMEM((16, width), BF16),
+            pltpu.VMEM((1, width), F32),
+            pltpu.VMEM((n_rows, 16), BF16),
+            pltpu.VMEM((n_rows, 128), F32),
             pltpu.VMEM((512, 256), BF16),
             pltpu.VMEM((128, 128), F32),
-            pltpu.VMEM((here + BLK, width), BF16),
-            pltpu.VMEM((n_rows, here + BLK), BF16),
+            *([pltpu.VMEM((BLK, width), BF16)] * 3),
+            *([pltpu.VMEM((n_rows, BLK), BF16)] * 3),
             pltpu.VMEM((here, width), BF16),
             pltpu.VMEM((n_rows, here), BF16),
             pltpu.VMEM((256, 256), F32),

time: 102 us -> 89.9 us (0.88)
  Pallas kernels: 95.5 us -> 83.3 us
    pallas_call x1, Pallas kernels: 34.3 us -> 22.1 us  [on_device(): pl.pallas_call(tile_kernel, out_shape=(jax.ShapeDtypeStruct((16, B), F32)...]
where the time goes in v3:
time: 89.9 us; the launch traced here: 89.6 us
  Pallas kernels  83.3 us (93%)
  local copies, waits for them, and re-layouts  5.65 us (6%)
    pallas_call x1, Pallas kernels, on_device(): pl.pallas_call(final_kernel, out_shape=(jax.ShapeDtypeStruct((64, B), F32...  49.3 us
    pallas_call x1, Pallas kernels, on_device(): pl.pallas_call(tile_kernel, out_shape=(jax.ShapeDtypeStruct((16, B), F32)...  22.1 us
    pallas_call x1, Pallas kernels, on_device(): pl.pallas_call(phase_kernel, out_shape=(jax.ShapeDtypeStruct((256, 128),...  11.9 us
    unnamed x5, local copies, waits for them, and re-layouts  5.12 us

profile of v3, /device:TPU:1, one launch (start us, length us, event | category | flops | bytes accessed | tf_op | source)
XLA Modules:
  0.0 89.6 jit_solution(3798585409459240891)
XLA Ops:
  0.6 0.0 copy-start
  0.6 0.6 copy-done
  1.3 0.5 pad.4.ridge_ref
  1.8 1.3 %copy.9 = s32[1,2,16,128]{3,2,1,0:T(8,128)} copy(s32[1,2,16,128]{3,1,2,0:T(2,128)} %bitcast.11) | data formatting | bytes 32768
  3.1 11.9 %phases.1 = (f32[256,128]{1,0:T(8,128)}, f32[1,128]{1,0:T(1,128)}) custom-call(s32[2,16,128]{2,1,0:T(8,128)} %bitcast.8, f32[1,128]{1,0:T(1,128)} %pad.4.ridge_ref), custom_call_target="tpu_custom_call" | custom-call | tf_op jit(solution)/shard_map/phases/pallas_call | solution.py:397
  15.0 22.1 %tile.1 = (f32[16,256]{1,0:T(8,128)}, f32[16,1024]{1,0:T(8,128)}, f32[4,64,256]{2,1,0:T(8,128)}, bf16[4,64,1024]{2,1,0:T(8,128)(2,1)}, f32[64,1024]{1,0:T(8,128)}) custom-call(f32[256,128]{1,0:T(8,128)} %get-tuple-element.9.phase_ref, s32[32,128]{1,0:T(8,128)} %bitcast.9, f32[32,128]{1,0:T(8,128)} %bitcast.10, f32[2,128]{1,0:T(2,128)} %bitcast.12), custom_call_target="tpu_custom_call" | custom-call | tf_op jit(solution)/shard_map/tile/pallas_call | solution.py:415
  37.1 49.3 %final.1 = (f32[64,256]{1,0:T(8,128)}, f32[64,1024]{1,0:T(8,128)}) custom-call(f32[16,256]{1,0:T(8,128)} %get-tuple-element.10.la_ref, f32[16,1024]{1,0:T(8,128)} %get-tuple-element.11.lb_ref, f32[4,64,256]{2,1,0:T(8,128)} %get-tuple-element.12.oa_ref, bf16[4,64,1024]{2,1,0:T(8,128)(2,1)} %get-tuple-element.13.ob_ref, f32[64,1024]{1,0:T(8,128)} %get-tuple-element.14.oc_ref, ...), custom_call_target="tpu_custom_call" | custom-call | tf_op jit(solution)/shard_map/final/pallas_call | solution.py:442
  86.4 1.5 %copy.12 = f32[64,256]{1,0:T(8,128)} copy(f32[64,256]{1,0:T(8,128)} %get-tuple-element.18) | data formatting | bytes 131072
  87.9 1.7 %copy.13 = f32[64,1024]{1,0:T(8,128)} copy(f32[64,1024]{1,0:T(8,128)} %get-tuple-element.19) | data formatting | bytes 524288
Async XLA Ops:
  0.6 0.7 copy-start

commit v4 on v3

--- a/solution.py
+++ b/solution.py
@@ -13,6 +13,7 @@
 HIGH = lax.Precision.HIGHEST
 B = 256
 BLK = 256
+CHUNK = 64
 PERIOD = 4096
 NX = 4
 WAVE = (8.88573567404434, -58.45953046181323, 115.03267724691959, -100.39492606524867)
@@ -89,9 +90,9 @@
     whole = (turn + ROUND) - ROUND
     z = 0.25 - jnp.abs(turn - whole)
     s = z * z
-    poly = WAVE[3]
-    for c in (WAVE[2], WAVE[1], WAVE[0]):
-        poly = poly * s + c
+    poly = s + WAVE[2] / WAVE[3]
+    for c in (WAVE[1], WAVE[0]):
+        poly = poly * s + c / WAVE[3]
     return poly * (z * scale)
 
 
@@ -122,7 +123,7 @@
         rows = jnp.concatenate(
             [order, order, degree, degree, shift, jnp.zeros((11, 128), F32)], axis=0
         )
-        return rows, scale_ref[pl.ds(k, 1), :]
+        return rows, scale_ref[pl.ds(k, 1), :] * WAVE[3]
 
     def down(row):
         return jnp.transpose(jnp.broadcast_to(row, (128, 128)))
@@ -161,36 +162,42 @@
             )
             parts += list(halves(q))
         parts += [jnp.ones((1, BLK), F32), jnp.zeros((11, BLK), F32)]
-        return jnp.concatenate(parts, axis=0).astype(BF16)
-
-    def design(qf, slot, j0):
-        turn = lax.dot_general(
-            qf, colf[:, j0 : j0 + 256], (((0,), (0,)), ((), ())), preferred_element_type=F32
+        rows = jnp.concatenate(parts, axis=0)
+        return rows.astype(BF16), jnp.transpose(rows).astype(BF16)
+
+    def design(qt, slot, j0):
+        scale = cols_s[:, j0 : j0 + 256]
+        for r0 in range(0, BLK, CHUNK):
+            turn = jnp.dot(
+                qt[r0 : r0 + CHUNK, :], colf[:, j0 : j0 + 256], preferred_element_type=F32
+            )
+            dcol[slot][r0 : r0 + CHUNK, j0 : j0 + 256] = wave(turn, scale).astype(BF16)
+
+    def design_rows(qf, slot):
+        for r0 in range(0, n_rows, CHUNK):
+            r1 = min(r0 + CHUNK, n_rows)
+            turn = jnp.dot(rowf[r0:r1, :], qf, preferred_element_type=F32)
+            scale = rows_s[r0:r1, :]
+            d = wave(turn, jnp.concatenate([scale, scale], axis=1))
+            drow[slot][r0:r1, :] = d.astype(BF16)
+
+    def filter_cols(b, s0, s1, j0):
+        both = jnp.concatenate(
+            [dcol[s0][:, j0 : j0 + 256], dcol[s1][:, j0 : j0 + 256]], axis=0
         )
-        d = wave(turn, cols_s[:, j0 : j0 + 256])
-        dcol[slot][:, j0 : j0 + 256] = d.astype(BF16)
-
-    def design_rows(qf, slot):
-        turn = jnp.dot(rowf[...], qf, preferred_element_type=F32)
-        scale = rows_s[...]
-        d = wave(turn, jnp.concatenate([scale, scale], axis=1))
-        drow[slot][...] = d.astype(BF16)
-
-    def filter_cols(b, s0, s1, j0):
-        f = jnp.dot(low_up[:, :BLK], dcol[s0][:, j0 : j0 + 256], preferred_element_type=F32)
-        f = f + jnp.dot(low_up[:, BLK:], dcol[s1][:, j0 : j0 + 256], preferred_element_type=F32)
+        f = jnp.dot(low_up, both, preferred_element_type=F32)
         fcol[pl.ds(pl.multiple_of(b * BLK, BLK), BLK), j0 : j0 + 256] = f.astype(BF16)
 
     def filter_rows(b, s0, s1):
-        f = jnp.dot(drow[s0][...], lowt[:BLK, :], preferred_element_type=F32)
-        f = f + jnp.dot(drow[s1][...], lowt[BLK:, :], preferred_element_type=F32)
+        both = jnp.concatenate([drow[s0][...], drow[s1][...]], axis=1)
+        f = jnp.dot(both, lowt[...], preferred_element_type=F32)
         frow[:, pl.ds(pl.multiple_of(b * BLK, BLK), BLK)] = f.astype(BF16)
 
     wide = range(0, n_tiles * 128, 256)
     for b in range(2):
-        qf = phases_of(b)
+        qf, qt = phases_of(b)
         for j0 in wide:
-            design(qf, b, j0)
+            design(qt, b, j0)
         design_rows(qf, b)
 
     @pl.when(x == 0)
@@ -202,10 +209,10 @@
     def _(step):
         for s in range(3):
             b = step * 3 + s
-            qf = phases_of(b + 2)
+            qf, qt = phases_of(b + 2)
             for j0 in wide:
                 filter_cols(b, s, (s + 1) % 3, j0)
-                design(qf, (s + 2) % 3, j0)
+                design(qt, (s + 2) % 3, j0)
             filter_rows(b, s, (s + 1) % 3)
             design_rows(qf, (s + 2) % 3)
 
@@ -243,22 +250,41 @@
 
 
 def block_inverse(a):
-    sub = lax.broadcasted_iota(jnp.int32, (NB, 1), 0)
-    lane = lax.broadcasted_iota(jnp.int32, (NB, NB), 1)
-    row = lax.broadcasted_iota(jnp.int32, (NB, NB), 0)
-    eye = jnp.where(lane == row, 1.0, 0.0).astype(F32)
-    m = jnp.concatenate([a, eye, jnp.zeros((NB, 128 - 2 * NB), F32)], axis=1)
+    groups = NB // 8
+    full = (8, 128)
+    sub = lax.broadcasted_iota(jnp.int32, full, 0)
+    lane = lax.broadcasted_iota(jnp.int32, full, 1)
+
+    def spread(v, s):
+        return jnp.broadcast_to(v[s : s + 1, :], full)
+
+    col = [
+        {k: jnp.broadcast_to(a[8 * k : 8 * k + 8, c : c + 1], full) for k in range(c // 8, groups)}
+        for c in range(NB)
+    ]
+    inv = [jnp.where(lane == sub + 8 * k, 1.0, 0.0).astype(F32) for k in range(groups)]
+    root = [jnp.zeros(full, F32) for _ in range(groups)]
     for i in range(NB):
-        top = m[i : i + 1, :]
-        scaled = top * (1.0 / top[:, i : i + 1])
-        m = m - jnp.where(sub > i, m[:, i : i + 1], 0.0) * scaled
-    diag = jnp.sum(m[:, :NB] * eye, axis=1, keepdims=True)
-    return m[:, NB : 2 * NB] * lax.rsqrt(diag)
+        k0, s = divmod(i, 8)
+        pivot = spread(col[i][k0], s)
+        over = 1.0 / pivot
+        root[k0] = jnp.where(sub == s, lax.rsqrt(pivot), root[k0])
+        ratio = {k: col[i][k] * over for k in range(k0, groups)}
+        ratio[k0] = jnp.where(sub > s, ratio[k0], 0.0)
+        for c in range(i + 1, NB):
+            kc, sc = divmod(c, 8)
+            top = spread(col[i][kc], sc)
+            for k in range(kc, groups):
+                col[c][k] = col[c][k] - ratio[k] * top
+        top = spread(inv[k0], s)
+        for k in range(k0, groups):
+            inv[k] = inv[k] - ratio[k] * top
+    return jnp.concatenate([inv[k] * root[k] for k in range(groups)], axis=0)
 
 
 def final_kernel(
     la_ref, lb_ref, oa_ref, ob_ref, oc_ref, ridge0_ref, ridge_ref, panel_ref, schur_ref,
-    slab_a, slab_b, got_la, got_lb, got_oa, got_ob, ridge4, ridge_far, mat,
+    slab_a, slab_b, got_la, got_lb, got_oa, got_ob, ridge4, ridge_far, mat, nxt_ref,
     s_la, r_la, s_lb, r_lb, s_oa, r_oa, s_ob, r_ob, s_r, r_r, s_f, r_f,
     s_za, r_za, s_zb, r_zb, s_ca, r_ca, s_cb, r_cb,
 ):
@@ -273,10 +299,12 @@
     barrier = pltpu.get_barrier_semaphore()
     peers = [device((x + i) % NX, z, core) for i in range(1, NX)]
     tall = [device(x, (z + i) % nz, core) for i in range(1, nz)]
+    far = [device((x + i) % NX, (z + 4) % nz, core) for i in range(NX)]
     other = device(x, z, 1 - core)
-    for peer in peers + tall + [other]:
+    greeted = peers + tall + far[1:] + [other]
+    for peer in greeted:
         pl.semaphore_signal(barrier, inc=1, device_id=peer, device_id_type=MESH)
-    pl.semaphore_wait(barrier, len(peers) + len(tall) + 1)
+    pl.semaphore_wait(barrier, len(greeted))
 
     def put(src, dst, send, recv, peer):
         copy = pltpu.make_async_remote_copy(
@@ -300,6 +328,8 @@
     ridges = [
         put(ridge0_ref, ridge4.at[x], s_r.at[i - 1], r_r.at[i - 1], peers[i - 1])
         for i in range(1, NX)
+    ] + [
+        put(ridge0_ref, ridge_far.at[x], s_f.at[i], r_f.at[i], far[i]) for i in range(NX)
     ]
     lead_b = to_x(lambda i: lb_ref, got_lb, s_lb, r_lb)
     ridge4[x] = ridge0_ref[...]
@@ -308,12 +338,9 @@
     slab_a[g] = la_ref[...] + got_la[0] + got_la[1] + got_la[2]
     z_a = to_z(slab_a, s_za, r_za)
     c_a = [to_core(slab_a, s_ca, r_ca, 0)]
-    for copy in ridges:
-        copy.wait()
-    far = put(ridge4, ridge_far, s_f, r_f, device(x, (z + 4) % nz, core))
     for copy in lead_b:
         copy.wait()
-    slab_b[g] = lb_ref[...] + got_lb[0] + got_lb[1] + got_lb[2]
+    slab_b[g] = (lb_ref[...] + got_lb[0] + got_lb[1] + got_lb[2]).astype(BF16)
     z_b = to_z(slab_b, s_zb, r_zb)
     c_b = [to_core(slab_b, s_cb, r_cb, 0)]
     own_a = to_x(lambda i: oa_ref.at[(x + i) % NX], got_oa, s_oa, r_oa)
@@ -321,8 +348,7 @@
     for i in range(1, nz):
         z_a[i - 1].wait()
         c_a.append(to_core(slab_a, s_ca, r_ca, i))
-    far.wait()
-    for copy in c_a:
+    for copy in c_a + ridges:
         copy.wait()
 
     lane = lax.broadcasted_iota(jnp.int32, (64, B), 1)
@@ -337,28 +363,32 @@
         mat[64 * k : 64 * k + 64, 0:B] = rows + jnp.where(lane == sub + 64 * k, lead_ridge[k], 0.0)
         mat[64 * k : 64 * k + 64, B:] = jnp.where(lane == sub + 64 * k, 1.0, 0.0).astype(F32)
 
-    nxt = mat[0:NB, 0:NB]
-    for j in range(B // NB):
-        if j == B // NB // 2:
-            for i in range(1, nz):
-                z_b[i - 1].wait()
-                c_b.append(to_core(slab_b, s_cb, r_cb, i))
-        r0, r1 = NB * j, NB * j + NB
-        w = block_inverse(nxt)
-        rj = dot(w, mat[r0:r1, :])
-        mat[r0:r1, :] = rj
-        if r1 < B:
-            hi, mid, low = split3(rj)
-            left = jnp.concatenate([hi, hi, mid, hi, low, mid], axis=0)
-            right = jnp.concatenate([hi, mid, hi, low, hi, mid], axis=0)
-            dims = (((0,), (0,)), ((), ()))
-            c0 = (r1 // 128) * 128
-            at = lax.dot_general(left[:, c0:B], right[:, c0:B], dims, preferred_element_type=F32)
-            nxt = mat[r1 : r1 + NB, r1 : r1 + NB] - at[r1 - c0 : r1 - c0 + NB, r1 - c0 : r1 - c0 + NB]
-            mat[r1:B, c0:B] -= at[r1 - c0 :, :]
-            w1 = B + ((r1 + 127) // 128) * 128
-            aw = lax.dot_general(left[:, c0:B], right[:, B:w1], dims, preferred_element_type=F32)
-            mat[r1:B, B:w1] -= aw[r1 - c0 :, :]
+    nxt_ref[...] = mat[0:NB, 0:128]
+    wide = lax.broadcasted_iota(jnp.int32, (NB, B), 1)
+
+    def block_step(j, carry):
+        r0 = pl.multiple_of(j * NB, NB)
+        r1 = r0 + NB
+        w = block_inverse(nxt_ref[:, 0:NB])[:, 0:NB]
+        rj = dot(w, mat[pl.ds(r0, NB), :])
+        mat[pl.ds(r0, NB), :] = rj
+        hi, mid, low = split3(rj)
+        right = jnp.concatenate([hi, mid, hi, low, hi, mid], axis=0)
+        hi, mid, low = split3(jnp.where(wide >= r1, rj[:, 0:B], 0.0))
+        left = jnp.concatenate([hi, hi, mid, hi, low, mid], axis=0)
+        mat[...] -= lax.dot_general(
+            left, right, (((0,), (0,)), ((), ())), preferred_element_type=F32
+        )
+        r1 = pl.multiple_of(jnp.minimum(r1, B - NB), NB)
+        nxt_ref[...] = pltpu.roll(mat[pl.ds(r1, NB), 0:B], B - r1, 1)[:, 0:128]
+        return carry
+
+    half = B // NB // 2
+    lax.fori_loop(0, half, block_step, 0)
+    for i in range(1, nz):
+        z_b[i - 1].wait()
+        c_b.append(to_core(slab_b, s_cb, r_cb, i))
+    lax.fori_loop(half, 2 * half, block_step, 0)
 
     for copy in own_a:
         copy.wait()
@@ -375,10 +405,14 @@
         copy.wait()
     cols = lb_ref.shape[1]
     for j0 in range(0, cols, B):
-        here = slab_b[:, :, j0 : j0 + B].reshape(B, B)
+        here = slab_b[:, :, j0 : j0 + B].reshape(B, B).astype(F32)
         if j0 == 0:
-            add = [jnp.where((lane == sub + 64 * k) & (y == 0), lead_ridge[k], 0.0) for k in range(4)]
-            here = here + jnp.concatenate(add, axis=0)
+            exact = [
+                slab_a[4 * k : 4 * k + 4].reshape(64, B)
+                + jnp.where(lane == sub + 64 * k, lead_ridge[k], 0.0)
+                for k in range(4)
+            ]
+            here = jnp.where(y == 0, jnp.concatenate(exact, axis=0), here)
         right = dot(winv, here)
         at = slice(j0, j0 + B)
         tile = oc_ref[:, at] + got_ob[0, :, at].astype(F32)
@@ -449,7 +483,7 @@
         out_specs=(VMEM, VMEM),
         scratch_shapes=[
             pltpu.VMEM((16, 16, B), F32),
-            pltpu.VMEM((16, 16, cols), F32),
+            pltpu.VMEM((16, 16, cols), BF16),
             pltpu.VMEM((NX - 1, 16, B), F32),
             pltpu.VMEM((NX - 1, 16, cols), F32),
             pltpu.VMEM((NX - 1, 64, B), F32),
@@ -457,7 +491,8 @@
             pltpu.VMEM((NX, 1, 128), F32),
             pltpu.VMEM((NX, 1, 128), F32),
             pltpu.VMEM((B, 2 * B), F32),
-            *([dma((3,))] * 10), dma, dma, *([dma((7,))] * 4), *([dma((8,))] * 4),
+            pltpu.VMEM((NB, 128), F32),
+            *([dma((3,))] * 10), dma((4,)), dma((4,)), *([dma((7,))] * 4), *([dma((8,))] * 4),
         ],
         compiler_params=pltpu.CompilerParams(collective_id=1, has_side_effects=True),
         name="final",

time: 89.9 us -> 73.1 us (0.81)
  Pallas kernels: 83.3 us -> 66.5 us
    pallas_call x1, Pallas kernels: 49.3 us -> 32.8 us  [on_device(): pl.pallas_call(final_kernel, out_shape=(jax.ShapeDtypeStruct((64, B), F32...]
where the time goes in v4:
time: 73.1 us; the launch traced here: 72.8 us
  Pallas kernels  66.5 us (91%)
  local copies, waits for them, and re-layouts  5.65 us (8%)
    pallas_call x1, Pallas kernels, on_device(): pl.pallas_call(final_kernel, out_shape=(jax.ShapeDtypeStruct((64, B), F32...  32.8 us
    pallas_call x1, Pallas kernels, on_device(): pl.pallas_call(tile_kernel, out_shape=(jax.ShapeDtypeStruct((16, B), F32)...  21.8 us
    pallas_call x1, Pallas kernels, on_device(): pl.pallas_call(phase_kernel, out_shape=(jax.ShapeDtypeStruct((256, 128),...  11.9 us
    unnamed x5, local copies, waits for them, and re-layouts  5.12 us

profile of v4, /device:TPU:1, one launch (start us, length us, event | category | flops | bytes accessed | tf_op | source)
XLA Modules:
  0.0 72.8 jit_solution(11183431741658649418)
XLA Ops:
  0.6 0.0 copy-start
  0.6 0.6 copy-done
  1.3 0.5 pad.4.ridge_ref
  1.8 1.3 %copy.9 = s32[1,2,16,128]{3,2,1,0:T(8,128)} copy(s32[1,2,16,128]{3,1,2,0:T(2,128)} %bitcast.11) | data formatting | bytes 32768
  3.1 11.9 %phases.1 = (f32[256,128]{1,0:T(8,128)}, f32[1,128]{1,0:T(1,128)}) custom-call(s32[2,16,128]{2,1,0:T(8,128)} %bitcast.8, f32[1,128]{1,0:T(1,128)} %pad.4.ridge_ref), custom_call_target="tpu_custom_call" | custom-call | tf_op jit(solution)/shard_map/phases/pallas_call | solution.py:431
  15.0 21.8 %tile.1 = (f32[16,256]{1,0:T(8,128)}, f32[16,1024]{1,0:T(8,128)}, f32[4,64,256]{2,1,0:T(8,128)}, bf16[4,64,1024]{2,1,0:T(8,128)(2,1)}, f32[64,1024]{1,0:T(8,128)}) custom-call(f32[256,128]{1,0:T(8,128)} %get-tuple-element.9.phase_ref, s32[32,128]{1,0:T(8,128)} %bitcast.9, f32[32,128]{1,0:T(8,128)} %bitcast.10, f32[2,128]{1,0:T(2,128)} %bitcast.12), custom_call_target="tpu_custom_call" | custom-call | tf_op jit(solution)/shard_map/tile/pallas_call | solution.py:449
  36.8 32.8 %final.1 = (f32[64,256]{1,0:T(8,128)}, f32[64,1024]{1,0:T(8,128)}) custom-call(f32[16,256]{1,0:T(8,128)} %get-tuple-element.10.la_ref, f32[16,1024]{1,0:T(8,128)} %get-tuple-element.11.lb_ref, f32[4,64,256]{2,1,0:T(8,128)} %get-tuple-element.12.oa_ref, bf16[4,64,1024]{2,1,0:T(8,128)(2,1)} %get-tuple-element.13.ob_ref, f32[64,1024]{1,0:T(8,128)} %get-tuple-element.14.oc_ref, ...), custom_call_target="tpu_custom_call" | custom-call | tf_op jit(solution)/shard_map/final/pallas_call | solution.py:476
  69.6 1.5 %copy.12 = f32[64,256]{1,0:T(8,128)} copy(f32[64,256]{1,0:T(8,128)} %get-tuple-element.18) | data formatting | bytes 131072
  71.1 1.7 %copy.13 = f32[64,1024]{1,0:T(8,128)} copy(f32[64,1024]{1,0:T(8,128)} %get-tuple-element.19) | data formatting | bytes 524288
Async XLA Ops:
  0.6 0.7 copy-start

commit v5 on v4

v5 whole, which is shorter than its diff:
```python
import functools

import jax
import jax.numpy as jnp
from jax import lax
from jax.experimental import pallas as pl
from jax.experimental.pallas import tpu as pltpu
from jax.sharding import PartitionSpec as P

F32 = jnp.float32
BF16 = jnp.bfloat16
MESH = pl.DeviceIdType.MESH
HIGH = lax.Precision.HIGHEST
B = 256
BLK = 256
CHUNK = 64
PERIOD = 4096
NX = 4
WAVE = (8.88573567404434, -58.45953046181323, 115.03267724691959, -100.39492606524867)
ROUND = 12582912.0
VMEM = pl.BlockSpec(memory_space=pltpu.VMEM)


def place():
    e, p, y = (lax.axis_index(a) for a in ("epoch", "prow", "pcol"))
    core, z_lo = e % 2, e // 2
    x, z_hi = p % NX, p // NX
    return x, y, z_hi * 4 + z_lo, core


def device(x, z, core):
    return {"epoch": (z % 4) * 2 + core, "prow": (z // 4) * NX + x}


def wave(turn, scale):
    whole = (turn + ROUND) - ROUND
    z = 0.25 - jnp.abs(turn - whole)
    s = z * z
    poly = s + WAVE[2] / WAVE[3]
    for c in (WAVE[1], WAVE[0]):
        poly = poly * s + c / WAVE[3]
    return poly * (z * scale)


def halves(v):
    hi = jnp.floor(v * 64.0) * (1.0 / 64.0)
    return hi, v - hi


def dot(a, b, dims=((1,), (0,))):
    return lax.dot_general(a, b, (dims, ((), ())), precision=HIGH, preferred_element_type=F32)


def split3(v):
    hi = v.astype(BF16)
    v = v - hi.astype(F32)
    mid = v.astype(BF16)
    low = (v - mid.astype(F32)).astype(BF16)
    return hi, mid, low


NB = 32


def block_inverse(a):
    groups = NB // 8
    full = (8, 128)
    sub = lax.broadcasted_iota(jnp.int32, full, 0)
    lane = lax.broadcasted_iota(jnp.int32, full, 1)

    def spread(v, s):
        return jnp.broadcast_to(v[s : s + 1, :], full)

    col = [
        {k: jnp.broadcast_to(a[8 * k : 8 * k + 8, c : c + 1], full) for k in range(c // 8, groups)}
        for c in range(NB)
    ]
    inv = [jnp.where(lane == sub + 8 * k, 1.0, 0.0).astype(F32) for k in range(groups)]
    root = [jnp.zeros(full, F32) for _ in range(groups)]
    for i in range(NB):
        k0, s = divmod(i, 8)
        pivot = spread(col[i][k0], s)
        over = 1.0 / pivot
        root[k0] = jnp.where(sub == s, lax.rsqrt(pivot), root[k0])
        ratio = {k: col[i][k] * over for k in range(k0, groups)}
        ratio[k0] = jnp.where(sub > s, ratio[k0], 0.0)
        for c in range(i + 1, NB):
            kc, sc = divmod(c, 8)
            top = spread(col[i][kc], sc)
            for k in range(kc, groups):
                col[c][k] = col[c][k] - ratio[k] * top
        top = spread(inv[k0], s)
        for k in range(k0, groups):
            inv[k] = inv[k] - ratio[k] * top
    return jnp.concatenate([inv[k] * root[k] for k in range(groups)], axis=0)


def whole_kernel(
    steps_ref, harm_ref, scale_ref, taps_ref, ridge_ref, out_ref,
    every, every_ridge, phase_ref,
    colf, cols_s, rowf, rows_s, lowt, lowr, d0, d1, d2, e0, e1, e2, fcol, frow, held,
    la_ref, lb_ref, oa_ref, ob_ref, oc_ref,
    slab_a, slab_b, got_la, got_lb, got_oa, got_ob, ridge4, ridge_far, mat, nxt_ref,
    s_st, r_st, s_ri, r_ri,
    s_la, r_la, s_lb, r_lb, s_oa, r_oa, s_ob, r_ob, s_r, r_r, s_f, r_f,
    s_za, r_za, s_zb, r_zb, s_ca, r_ca, s_cb, r_cb,
):
    x, y, z, core = place()
    e, p = lax.axis_index("epoch"), lax.axis_index("prow")
    nz, ne = 8, 8

    def group(zz, cc):
        return ((zz % 4) * 2 + cc) * 2 + zz // 4

    g = group(z, core)
    peers = [device((x + i) % NX, z, core) for i in range(1, NX)]
    tall = [device(x, (z + i) % nz, core) for i in range(1, nz)]
    ring = [{"epoch": (e + i) % ne} for i in range(1, ne)]
    across = [device(x, (1 - z // 4) * 4 + i, core) for i in range(4)]
    other = device(x, z, 1 - core)
    barrier = pltpu.get_barrier_semaphore()
    greeted = ring + peers + across
    for peer in greeted:
        pl.semaphore_signal(barrier, inc=1, device_id=peer, device_id_type=MESH)
    pl.semaphore_wait(barrier, len(greeted))

    def put(src, dst, send, recv, peer):
        copy = pltpu.make_async_remote_copy(
            src_ref=src, dst_ref=dst, send_sem=send, recv_sem=recv,
            device_id=peer, device_id_type=MESH,
        )
        copy.start()
        return copy

    def to_x(src, got, send, recv):
        return [put(src(i), got.at[i - 1], send.at[i - 1], recv.at[i - 1], peers[i - 1]) for i in range(1, NX)]

    def to_z(slab, send, recv):
        return [put(slab.at[g], slab.at[g], send.at[i - 1], recv.at[i - 1], tall[i - 1]) for i in range(1, nz)]

    def to_core(slab, send, recv, i):
        k = group((z + nz - i) % nz, core)
        return put(slab.at[k], slab.at[k], send.at[i], recv.at[i], other)

    given = [
        put(steps_ref, every.at[e], s_st.at[i], r_st.at[i], ring[i]) for i in range(ne - 1)
    ] + [
        put(ridge_ref, every_ridge.at[e], s_ri.at[i], r_ri.at[i], ring[i]) for i in range(ne - 1)
    ]
    every[e] = steps_ref[...]
    every_ridge[e] = ridge_ref[...]
    blocks = (ne * steps_ref.shape[1] // BLK) // NX
    n_rows = rows_s.shape[0]
    n_lead = n_rows - 256
    n_tiles = colf.shape[1] // 128
    cols_here = n_tiles - 2
    dcol, drow = (d0, d1, d2), (e0, e1, e2)

    def features(k):
        h = harm_ref[pl.ds(k, 1), :]
        order = lax.shift_right_logical(h, 6).astype(F32)
        degree = (h & 63).astype(F32)
        shift = jnp.full((1, 128), -0.125, F32)
        rows = jnp.concatenate(
            [order, order, degree, degree, shift, jnp.zeros((11, 128), F32)], axis=0
        )
        return rows, scale_ref[pl.ds(k, 1), :] * WAVE[3]

    def down(row):
        return jnp.transpose(jnp.broadcast_to(row, (128, 128)))

    for jt in range(n_tiles):
        k = jt if jt < 2 else y * cols_here + (jt - 2)
        rows, scale = features(k)
        colf[:, jt * 128 : jt * 128 + 128] = rows.astype(BF16)
        cols_s[:, jt * 128 : jt * 128 + 128] = scale
    for half in range(2):
        rows, scale = features(g * 2 + half)
        rowf[half * 128 : half * 128 + 128, :] = jnp.transpose(rows).astype(BF16)
        rows_s[half * 128 : half * 128 + 128, :] = down(scale)
    per = 128 // n_lead
    rows, scale = features(g // per)
    piece = pl.ds(pl.multiple_of((g % per) * n_lead, n_lead), n_lead)
    lowr[...] = down(scale)
    rows_s[256:, :] = lowr[piece, :]
    lowr[:, 0:16] = jnp.transpose(rows)
    rowf[256:, :] = lowr[piece, 0:16].astype(BF16)

    base = jnp.concatenate([taps_ref[0:1, :], taps_ref[1:2, :], jnp.zeros((1, 256), F32)], axis=1)
    full = pltpu.roll(
        jnp.broadcast_to(base, (512, 512)), 256, 1, stride=1, stride_axis=0
    )[:, :256]
    lowt[...] = full.astype(BF16)
    low_up = jnp.transpose(full).astype(BF16)


    pairs = 2 * ne
    rows = pairs * steps_ref.shape[1] // 128
    upper = (
        lax.broadcasted_iota(jnp.int32, (128, 128), 0)
        <= lax.broadcasted_iota(jnp.int32, (128, 128), 1)
    ).astype(BF16)
    r_at = lax.broadcasted_iota(jnp.int32, (rows, rows), 0)
    s_at = lax.broadcasted_iota(jnp.int32, (rows, rows), 1)
    same = r_at % 2 == s_at % 2
    key_r = ((r_at % pairs) // 2) * rows + r_at // pairs
    key_s = ((s_at % pairs) // 2) * rows + s_at // pairs
    before = jnp.where(same & (key_s < key_r), 1.0, 0.0).astype(BF16)
    for copy in given:
        copy.wait()
    flat = every[...].astype(F32).reshape(pairs, steps_ref.shape[1])
    stack = jnp.concatenate(
        [flat[:, 128 * k : 128 * k + 128] for k in range(rows // pairs)], axis=0
    )
    inside = jnp.dot(stack.astype(BF16), upper, preferred_element_type=F32)
    totals = jnp.broadcast_to(inside[:, 127:128], (rows, 128))
    high = jnp.floor(totals * (1.0 / 64.0))
    low = totals - high * 64.0
    earlier = jnp.dot(before, high.astype(BF16), preferred_element_type=F32) * 64.0
    earlier = earlier + jnp.dot(before, low.astype(BF16), preferred_element_type=F32)
    turns = (inside + earlier) * (1.0 / PERIOD)
    phase_ref[...] = turns - jnp.floor(turns)

    def phases_of(b):
        at = jnp.maximum(x * blocks + b - 1, 0)
        row0 = (at % 8) * 32 + (at // 8) * 2
        parts = []
        for a in range(2):
            q = jnp.concatenate(
                [phase_ref[pl.ds(row0 + 16 * half + a, 1), :] for half in range(2)], axis=1
            )
            parts += list(halves(q))
        parts += [jnp.ones((1, BLK), F32), jnp.zeros((11, BLK), F32)]
        rows = jnp.concatenate(parts, axis=0)
        return rows.astype(BF16), jnp.transpose(rows).astype(BF16)

    def design(qt, slot, j0):
        scale = cols_s[:, j0 : j0 + 256]
        for r0 in range(0, BLK, CHUNK):
            turn = jnp.dot(
                qt[r0 : r0 + CHUNK, :], colf[:, j0 : j0 + 256], preferred_element_type=F32
            )
            dcol[slot][r0 : r0 + CHUNK, j0 : j0 + 256] = wave(turn, scale).astype(BF16)

    def design_rows(qf, slot):
        for r0 in range(0, n_rows, CHUNK):
            r1 = min(r0 + CHUNK, n_rows)
            turn = jnp.dot(rowf[r0:r1, :], qf, preferred_element_type=F32)
            scale = rows_s[r0:r1, :]
            d = wave(turn, jnp.concatenate([scale, scale], axis=1))
            drow[slot][r0:r1, :] = d.astype(BF16)

    def filter_cols(b, s0, s1, j0):
        both = jnp.concatenate(
            [dcol[s0][:, j0 : j0 + 256], dcol[s1][:, j0 : j0 + 256]], axis=0
        )
        f = jnp.dot(low_up, both, preferred_element_type=F32)
        fcol[pl.ds(pl.multiple_of(b * BLK, BLK), BLK), j0 : j0 + 256] = f.astype(BF16)

    def filter_rows(b, s0, s1):
        both = jnp.concatenate([drow[s0][...], drow[s1][...]], axis=1)
        f = jnp.dot(both, lowt[...], preferred_element_type=F32)
        frow[:, pl.ds(pl.multiple_of(b * BLK, BLK), BLK)] = f.astype(BF16)

    wide = range(0, n_tiles * 128, 256)
    for b in range(2):
        qf, qt = phases_of(b)
        for j0 in wide:
            design(qt, b, j0)
        design_rows(qf, b)

    @pl.when(x == 0)
    def _():
        d0[...] = jnp.zeros_like(d0)
        e0[...] = jnp.zeros_like(e0)

    @pl.loop(0, blocks // 3)
    def _(step):
        for s in range(3):
            b = step * 3 + s
            qf, qt = phases_of(b + 2)
            for j0 in wide:
                filter_cols(b, s, (s + 1) % 3, j0)
                design(qt, (s + 2) % 3, j0)
            filter_rows(b, s, (s + 1) % 3)
            design_rows(qf, (s + 2) % 3)

    for b in range(blocks // 3 * 3, blocks):
        for j0 in wide:
            filter_cols(b, b % 3, (b + 1) % 3, j0)
        filter_rows(b, b % 3, (b + 1) % 3)

    total = 1.0 / (blocks * BLK * NX)

    def product(j0):
        return jnp.dot(frow[...], fcol[:, j0 : j0 + B], preferred_element_type=F32) * total

    part = product(0)
    la_ref[...] = part[B:]
    oa_ref[...] = part[:B].reshape(NX, 64, B)
    ridge4[x] = every_ridge[0]
    lead_a = to_x(lambda i: la_ref, got_la, s_la, r_la)
    ridges = [
        put(every_ridge.at[0], ridge4.at[x], s_r.at[i - 1], r_r.at[i - 1], peers[i - 1])
        for i in range(1, NX)
    ]
    for j0 in range(0, cols_here * 128, B):
        part = product(B + j0)
        at = slice(j0, j0 + B)
        lb_ref[:, at] = part[B:]
        held[...] = part[:B]
        ob_ref[:, :, at] = part[:B].astype(BF16).reshape(NX, 64, B)
        oc_ref[:, at] = held[pl.ds(pl.multiple_of(x * 64, 64), 64), :]
    lead_b = to_x(lambda i: lb_ref, got_lb, s_lb, r_lb)
    for copy in lead_a:
        copy.wait()
    slab_a[g] = la_ref[...] + got_la[0] + got_la[1] + got_la[2]
    z_a = to_z(slab_a, s_za, r_za)
    c_a = [to_core(slab_a, s_ca, r_ca, 0)]
    for copy in ridges:
        copy.wait()
    far = put(ridge4, ridge_far, s_f, r_f, device(x, (z + 4) % nz, core))
    own_a = to_x(lambda i: oa_ref.at[(x + i) % NX], got_oa, s_oa, r_oa)
    own_b = to_x(lambda i: ob_ref.at[(x + i) % NX], got_ob, s_ob, r_ob)
    for copy in lead_b:
        copy.wait()
    slab_b[g] = (lb_ref[...] + got_lb[0] + got_lb[1] + got_lb[2]).astype(BF16)
    z_b = to_z(slab_b, s_zb, r_zb)
    c_b = [to_core(slab_b, s_cb, r_cb, 0)]
    for i in range(1, nz):
        z_a[i - 1].wait()
        c_a.append(to_core(slab_a, s_ca, r_ca, i))
    far.wait()
    for copy in c_a:
        copy.wait()

    lane = lax.broadcasted_iota(jnp.int32, (64, B), 1)
    sub = lax.broadcasted_iota(jnp.int32, (64, B), 0)

    def column(row):
        return jnp.transpose(jnp.broadcast_to(row, (128, 64)))[:, 0:1]

    lead_ridge = [column(jnp.where(z < 4, ridge4[k], ridge_far[k])) for k in range(4)]
    for k in range(4):
        rows = slab_a[4 * k : 4 * k + 4].reshape(64, B)
        mat[64 * k : 64 * k + 64, 0:B] = rows + jnp.where(lane == sub + 64 * k, lead_ridge[k], 0.0)
        mat[64 * k : 64 * k + 64, B:] = jnp.where(lane == sub + 64 * k, 1.0, 0.0).astype(F32)

    nxt_ref[...] = mat[0:NB, 0:128]
    wide = lax.broadcasted_iota(jnp.int32, (NB, B), 1)

    def block_step(j, carry):
        r0 = pl.multiple_of(j * NB, NB)
        r1 = r0 + NB
        w = block_inverse(nxt_ref[:, 0:NB])[:, 0:NB]
        rj = dot(w, mat[pl.ds(r0, NB), :])
        mat[pl.ds(r0, NB), :] = rj
        hi, mid, low = split3(rj)
        right = jnp.concatenate([hi, mid, hi, low, hi, mid], axis=0)
        hi, mid, low = split3(jnp.where(wide >= r1, rj[:, 0:B], 0.0))
        left = jnp.concatenate([hi, hi, mid, hi, low, mid], axis=0)
        mat[...] -= lax.dot_general(
            left, right, (((0,), (0,)), ((), ())), preferred_element_type=F32
        )
        r1 = pl.multiple_of(jnp.minimum(r1, B - NB), NB)
        nxt_ref[...] = pltpu.roll(mat[pl.ds(r1, NB), 0:B], B - r1, 1)[:, 0:128]
        return carry

    half = B // NB // 2
    lax.fori_loop(0, half, block_step, 0)
    for i in range(1, nz):
        z_b[i - 1].wait()
        c_b.append(to_core(slab_b, s_cb, r_cb, i))
    lax.fori_loop(half, 2 * half, block_step, 0)

    for copy in own_a:
        copy.wait()
    first = (e * 8 + p) * 64
    own_ridge = column(ridge_ref[...])
    winv = mat[:, B:]
    lead = oa_ref[x] + got_oa[0] + got_oa[1] + got_oa[2]
    lead = lead + jnp.where(lane == sub + first, own_ridge, 0.0)
    panel = dot(lead, winv, ((1,), (1,)))
    out_ref[:, 0:B] = panel
    for copy in c_b:
        copy.wait()
    for copy in own_b:
        copy.wait()
    cols = lb_ref.shape[1]
    for j0 in range(0, cols, B):
        here = slab_b[:, :, j0 : j0 + B].reshape(B, B).astype(F32)
        if j0 == 0:
            exact = [
                slab_a[4 * k : 4 * k + 4].reshape(64, B)
                + jnp.where(lane == sub + 64 * k, lead_ridge[k], 0.0)
                for k in range(4)
            ]
            here = jnp.where(y == 0, jnp.concatenate(exact, axis=0), here)
        right = dot(winv, here)
        at = slice(j0, j0 + B)
        tile = oc_ref[:, at] + got_ob[0, :, at].astype(F32)
        tile = tile + got_ob[1, :, at].astype(F32) + got_ob[2, :, at].astype(F32)
        tile = tile + jnp.where(lane + (y * cols + j0) == sub + first, own_ridge, 0.0)
        out_ref[:, B + j0 : B + j0 + B] = tile - dot(panel, right)


def split_kernel(both_ref, panel_ref, schur_ref):
    panel_ref[...] = both_ref[:, 0:B]
    schur_ref[...] = both_ref[:, B:]


def on_device(steps, harmonic, col_scale, taps, ridge):
    cols = harmonic.shape[0] // 4
    width = cols + B
    here, n_rows = 4096, 272
    dma = pltpu.SemaphoreType.DMA
    vmem = pltpu.VMEM
    both = pl.pallas_call(
        whole_kernel,
        out_shape=jax.ShapeDtypeStruct((64, width), F32),
        in_specs=[VMEM] * 5,
        out_specs=VMEM,
        scratch_shapes=[
            vmem((8, 2, steps.shape[1]), jnp.int32),
            vmem((8, 1, 64), F32),
            vmem((256, 128), F32),
            vmem((16, width), BF16),
            vmem((1, width), F32),
            vmem((n_rows, 16), BF16),
            vmem((n_rows, 128), F32),
            vmem((512, 256), BF16),
            vmem((128, 128), F32),
            *([vmem((BLK, width), BF16)] * 3),
            *([vmem((n_rows, BLK), BF16)] * 3),
            vmem((here, width), BF16),
            vmem((n_rows, here), BF16),
            vmem((256, 256), F32),
            vmem((16, B), F32),
            vmem((16, cols), F32),
            vmem((NX, 64, B), F32),
            vmem((NX, 64, cols), BF16),
            vmem((64, cols), F32),
            vmem((16, 16, B), F32),
            vmem((16, 16, cols), BF16),
            vmem((NX - 1, 16, B), F32),
            vmem((NX - 1, 16, cols), F32),
            vmem((NX - 1, 64, B), F32),
            vmem((NX - 1, 64, cols), BF16),
            vmem((NX, 1, 64), F32),
            vmem((NX, 1, 64), F32),
            vmem((B, 2 * B), F32),
            vmem((NB, 128), F32),
            *([dma((7,))] * 4), *([dma((3,))] * 10), dma, dma,
            *([dma((7,))] * 4), *([dma((8,))] * 4),
        ],
        compiler_params=pltpu.CompilerParams(
            collective_id=0, has_side_effects=True, vmem_limit_bytes=60 * 1024 * 1024
        ),
        name="whole",
    )(
        steps,
        harmonic.reshape(-1, 128),
        col_scale.reshape(-1, 128),
        taps.reshape(2, 128),
        ridge.reshape(1, -1),
    )
    return pl.pallas_call(
        split_kernel,
        out_shape=(
            jax.ShapeDtypeStruct((64, B), F32),
            jax.ShapeDtypeStruct((64, cols), F32),
        ),
        in_specs=[VMEM],
        out_specs=(VMEM, VMEM),
        name="split",
    )(both)


def solution(mesh):
    row = P(("epoch", "prow"))
    return jax.shard_map(
        on_device,
        mesh=mesh,
        in_specs=(P(None, "epoch"), P(), P(), P(), row),
        out_specs=(P(("epoch", "prow"), None), P(("epoch", "prow"), "pcol")),
        check_vma=False,
    )
```

time: 73.1 us -> 59.7 us (0.82)
  Pallas kernels: 66.5 us -> 58.9 us
  local copies, waits for them, and re-layouts: 5.65 us -> 0 us
    pallas_call x3 -> x2, Pallas kernels: 66.5 us -> 58.9 us  [the longest x1 57.2 us: on_device(): pl.pallas_call(whole_kernel, out_shape=jax.ShapeDtypeStruct((64, width),...]
    unnamed x5 -> x0, local copies, waits for them, and re-layouts: 5.12 us -> none
where the time goes in v5:
time: 59.7 us; the launch traced here: 59.5 us
  Pallas kernels  58.9 us (99%)
  between operations  0.64 us (1%)
    pallas_call x1, Pallas kernels, on_device(): pl.pallas_call(whole_kernel, out_shape=jax.ShapeDtypeStruct((64, width),...  57.2 us
    pallas_call x1, Pallas kernels, on_device(): pl.pallas_call(split_kernel, out_shape=(jax.ShapeDtypeStruct((64, B), F32...  1.7 us

profile of v5, /device:TPU:1, one launch (start us, length us, event | category | flops | bytes accessed | tf_op | source)
XLA Modules:
  0.0 59.5 jit_solution(6494683811738262861)
XLA Ops:
  0.6 57.2 %whole.1.both_ref = f32[64,1280]{1,0:T(8,128)} custom-call(s32[2,2048]{1,0:T(2,128)} %steps_ref.1, s32[32,128]{1,0:T(8,128)} %bitcast.4, f32[32,128]{1,0:T(8,128)} %bitcast.5, f32[2,128]{1,0:T(2,128)} %bitcast.6, f32[1,64]{1,0:T(1,128)} %bitcast.7), custom_call_target="tpu_custom_call" | custom-call | tf_op jit(solution)/shard_map/whole/pallas_call | solution.py:418
  57.8 1.7 %split.1 = (f32[64,256]{1,0:T(8,128)}, f32[64,1024]{1,0:T(8,128)}) custom-call(f32[64,1280]{1,0:T(8,128)} %whole.1.both_ref), custom_call_target="tpu_custom_call" | custom-call | tf_op jit(solution)/shard_map/split/pallas_call | solution.py:467

commit v6 on v5

--- a/solution.py
+++ b/solution.py
@@ -98,10 +98,10 @@
 def whole_kernel(
     steps_ref, harm_ref, scale_ref, taps_ref, ridge_ref, out_ref,
     every, every_ridge, phase_ref,
-    colf, cols_s, rowf, rows_s, lowt, lowr, d0, d1, d2, e0, e1, e2, fcol, frow, held,
+    colf, cols_s, rowf, rows_s, lowt, lowr, d0, d1, d2, e0, e1, e2, fcol, frow, mine, theirs, got_p,
     la_ref, lb_ref, oa_ref, ob_ref, oc_ref,
     slab_a, slab_b, got_la, got_lb, got_oa, got_ob, ridge4, ridge_far, mat, nxt_ref,
-    s_st, r_st, s_ri, r_ri,
+    s_st, r_st, s_ri, r_ri, s_p, r_p,
     s_la, r_la, s_lb, r_lb, s_oa, r_oa, s_ob, r_ob, s_r, r_r, s_f, r_f,
     s_za, r_za, s_zb, r_zb, s_ca, r_ca, s_cb, r_cb,
 ):
@@ -149,9 +149,10 @@
     ]
     every[e] = steps_ref[...]
     every_ridge[e] = ridge_ref[...]
-    blocks = (ne * steps_ref.shape[1] // BLK) // NX
+    blocks = (ne * steps_ref.shape[1] // BLK) // (2 * NX)
     n_rows = rows_s.shape[0]
-    n_lead = n_rows - 256
+    n_side = n_rows // 2
+    n_lead = n_side - 256
     n_tiles = colf.shape[1] // 128
     cols_here = n_tiles - 2
     dcol, drow = (d0, d1, d2), (e0, e1, e2)
@@ -174,17 +175,21 @@
         rows, scale = features(k)
         colf[:, jt * 128 : jt * 128 + 128] = rows.astype(BF16)
         cols_s[:, jt * 128 : jt * 128 + 128] = scale
-    for half in range(2):
-        rows, scale = features(g * 2 + half)
-        rowf[half * 128 : half * 128 + 128, :] = jnp.transpose(rows).astype(BF16)
-        rows_s[half * 128 : half * 128 + 128, :] = down(scale)
     per = 128 // n_lead
-    rows, scale = features(g // per)
-    piece = pl.ds(pl.multiple_of((g % per) * n_lead, n_lead), n_lead)
-    lowr[...] = down(scale)
-    rows_s[256:, :] = lowr[piece, :]
-    lowr[:, 0:16] = jnp.transpose(rows)
-    rowf[256:, :] = lowr[piece, 0:16].astype(BF16)
+    for side, gg in enumerate((group(z, 1 - core), g)):
+        top = side * n_side
+        for half in range(2):
+            rows, scale = features(gg * 2 + half)
+            at = slice(top + half * 128, top + half * 128 + 128)
+            rowf[at, :] = jnp.transpose(rows).astype(BF16)
+            rows_s[at, :] = down(scale)
+        rows, scale = features(gg // per)
+        piece = pl.ds(pl.multiple_of((gg % per) * n_lead, n_lead), n_lead)
+        at = slice(top + 256, top + n_side)
+        lowr[...] = down(scale)
+        rows_s[at, :] = lowr[piece, :]
+        lowr[:, 0:16] = jnp.transpose(rows)
+        rowf[at, :] = lowr[piece, 0:16].astype(BF16)
 
     base = jnp.concatenate([taps_ref[0:1, :], taps_ref[1:2, :], jnp.zeros((1, 256), F32)], axis=1)
     full = pltpu.roll(
@@ -222,7 +227,7 @@
     phase_ref[...] = turns - jnp.floor(turns)
 
     def phases_of(b):
-        at = jnp.maximum(x * blocks + b - 1, 0)
+        at = jnp.maximum((x * 2 + core) * blocks + b - 1, 0)
         row0 = (at % 8) * 32 + (at // 8) * 2
         parts = []
         for a in range(2):
@@ -269,33 +274,44 @@
             design(qt, b, j0)
         design_rows(qf, b)
 
-    @pl.when(x == 0)
+    @pl.when((x == 0) & (core == 0))
     def _():
         d0[...] = jnp.zeros_like(d0)
         e0[...] = jnp.zeros_like(e0)
 
-    @pl.loop(0, blocks // 3)
+    def block_pass(b, s, more):
+        if more:
+            qf, qt = phases_of(b + 2)
+        for j0 in wide:
+            filter_cols(b, s, (s + 1) % 3, j0)
+            if more:
+                design(qt, (s + 2) % 3, j0)
+        filter_rows(b, s, (s + 1) % 3)
+        if more:
+            design_rows(qf, (s + 2) % 3)
+
+    trips = (blocks - 1) // 3
+
+    @pl.loop(0, trips)
     def _(step):
         for s in range(3):
-            b = step * 3 + s
-            qf, qt = phases_of(b + 2)
-            for j0 in wide:
-                filter_cols(b, s, (s + 1) % 3, j0)
-                design(qt, (s + 2) % 3, j0)
-            filter_rows(b, s, (s + 1) % 3)
-            design_rows(qf, (s + 2) % 3)
-
-    for b in range(blocks // 3 * 3, blocks):
-        for j0 in wide:
-            filter_cols(b, b % 3, (b + 1) % 3, j0)
-        filter_rows(b, b % 3, (b + 1) % 3)
-
-    total = 1.0 / (blocks * BLK * NX)
-
-    def product(j0):
-        return jnp.dot(frow[...], fcol[:, j0 : j0 + B], preferred_element_type=F32) * total
-
-    part = product(0)
+            block_pass(step * 3 + s, s, True)
+
+    for b in range(trips * 3, blocks):
+        block_pass(b, b % 3, b + 2 <= blocks)
+
+    total = 1.0 / (blocks * BLK * 2 * NX)
+
+    def product(j):
+        at = slice(j * B, j * B + B)
+        part = jnp.dot(frow[...], fcol[:, at], preferred_element_type=F32) * total
+        theirs[j] = part[:n_side]
+        mine[j] = part[n_side:]
+        return put(theirs.at[j], got_p.at[j], s_p.at[j], r_p.at[j], other)
+
+    swaps = [product(0), product(1)]
+    swaps[0].wait()
+    part = mine[0] + got_p[0]
     la_ref[...] = part[B:]
     oa_ref[...] = part[:B].reshape(NX, 64, B)
     ridge4[x] = every_ridge[0]
@@ -304,13 +320,16 @@
         put(every_ridge.at[0], ridge4.at[x], s_r.at[i - 1], r_r.at[i - 1], peers[i - 1])
         for i in range(1, NX)
     ]
-    for j0 in range(0, cols_here * 128, B):
-        part = product(B + j0)
-        at = slice(j0, j0 + B)
+    own_piece = pl.ds(pl.multiple_of(x * 64, 64), 64)
+    for j in range(1, n_tiles // 2):
+        if j + 1 < n_tiles // 2:
+            swaps.append(product(j + 1))
+        swaps[j].wait()
+        part = mine[j] + got_p[j]
+        at = slice(j * B - B, j * B)
         lb_ref[:, at] = part[B:]
-        held[...] = part[:B]
         ob_ref[:, :, at] = part[:B].astype(BF16).reshape(NX, 64, B)
-        oc_ref[:, at] = held[pl.ds(pl.multiple_of(x * 64, 64), 64), :]
+        oc_ref[:, at] = mine[j, own_piece, :] + got_p[j, own_piece, :]
     lead_b = to_x(lambda i: lb_ref, got_lb, s_lb, r_lb)
     for copy in lead_a:
         copy.wait()
@@ -381,6 +400,8 @@
     lead = oa_ref[x] + got_oa[0] + got_oa[1] + got_oa[2]
     lead = lead + jnp.where(lane == sub + first, own_ridge, 0.0)
     panel = dot(lead, winv, ((1,), (1,)))
+    weight = dot(panel, winv)
+    parts = jnp.concatenate(split3(weight), axis=0)
     out_ref[:, 0:B] = panel
     for copy in c_b:
         copy.wait()
@@ -388,20 +409,22 @@
         copy.wait()
     cols = lb_ref.shape[1]
     for j0 in range(0, cols, B):
-        here = slab_b[:, :, j0 : j0 + B].reshape(B, B).astype(F32)
+        three = jnp.dot(
+            parts, slab_b[:, :, j0 : j0 + B].reshape(B, B), preferred_element_type=F32
+        )
+        known = three[0:64] + three[64:128] + three[128:192]
         if j0 == 0:
             exact = [
                 slab_a[4 * k : 4 * k + 4].reshape(64, B)
                 + jnp.where(lane == sub + 64 * k, lead_ridge[k], 0.0)
                 for k in range(4)
             ]
-            here = jnp.where(y == 0, jnp.concatenate(exact, axis=0), here)
-        right = dot(winv, here)
+            known = jnp.where(y == 0, dot(weight, jnp.concatenate(exact, axis=0)), known)
         at = slice(j0, j0 + B)
         tile = oc_ref[:, at] + got_ob[0, :, at].astype(F32)
         tile = tile + got_ob[1, :, at].astype(F32) + got_ob[2, :, at].astype(F32)
         tile = tile + jnp.where(lane + (y * cols + j0) == sub + first, own_ridge, 0.0)
-        out_ref[:, B + j0 : B + j0 + B] = tile - dot(panel, right)
+        out_ref[:, B + j0 : B + j0 + B] = tile - known
 
 
 def split_kernel(both_ref, panel_ref, schur_ref):
@@ -412,7 +435,7 @@
 def on_device(steps, harmonic, col_scale, taps, ridge):
     cols = harmonic.shape[0] // 4
     width = cols + B
-    here, n_rows = 4096, 272
+    here, n_rows = 2048, 544
     dma = pltpu.SemaphoreType.DMA
     vmem = pltpu.VMEM
     both = pl.pallas_call(
@@ -434,7 +457,7 @@
             *([vmem((n_rows, BLK), BF16)] * 3),
             vmem((here, width), BF16),
             vmem((n_rows, here), BF16),
-            vmem((256, 256), F32),
+            *([vmem((width // B, n_rows // 2, B), F32)] * 3),
             vmem((16, B), F32),
             vmem((16, cols), F32),
             vmem((NX, 64, B), F32),
@@ -450,7 +473,7 @@
             vmem((NX, 1, 64), F32),
             vmem((B, 2 * B), F32),
             vmem((NB, 128), F32),
-            *([dma((7,))] * 4), *([dma((3,))] * 10), dma, dma,
+            *([dma((7,))] * 4), *([dma((5,))] * 2), *([dma((3,))] * 10), dma, dma,
             *([dma((7,))] * 4), *([dma((8,))] * 4),
         ],
         compiler_params=pltpu.CompilerParams(

time: 59.7 us -> 55.7 us (0.933)
  Pallas kernels: 58.9 us -> 54.9 us
    pallas_call x1, Pallas kernels: 57.2 us -> 53.2 us  [on_device(): pl.pallas_call(whole_kernel, out_shape=jax.ShapeDtypeStruct((64, width),...]
where the time goes in v6:
time: 55.7 us; the launch traced here: 55.5 us
  Pallas kernels  54.9 us (99%)
  between operations  0.64 us (1%)
    pallas_call x1, Pallas kernels, on_device(): pl.pallas_call(whole_kernel, out_shape=jax.ShapeDtypeStruct((64, width),...  53.2 us
    pallas_call x1, Pallas kernels, on_device(): pl.pallas_call(split_kernel, out_shape=(jax.ShapeDtypeStruct((64, B), F32...  1.7 us

profile of v6, /device:TPU:1, one launch (start us, length us, event | category | flops | bytes accessed | tf_op | source)
XLA Modules:
  0.0 55.5 jit_solution(4125529222076471225)
XLA Ops:
  0.6 53.2 %whole.1.both_ref = f32[64,1280]{1,0:T(8,128)} custom-call(s32[2,2048]{1,0:T(2,128)} %steps_ref.1, s32[32,128]{1,0:T(8,128)} %bitcast.4, f32[32,128]{1,0:T(8,128)} %bitcast.5, f32[2,128]{1,0:T(2,128)} %bitcast.6, f32[1,64]{1,0:T(1,128)} %bitcast.7), custom_call_target="tpu_custom_call" | custom-call | tf_op jit(solution)/shard_map/whole/pallas_call | solution.py:441
  53.8 1.7 %split.1 = (f32[64,256]{1,0:T(8,128)}, f32[64,1024]{1,0:T(8,128)}) custom-call(f32[64,1280]{1,0:T(8,128)} %whole.1.both_ref), custom_call_target="tpu_custom_call" | custom-call | tf_op jit(solution)/shard_map/split/pallas_call | solution.py:490

commit v7 on v6

--- a/solution.py
+++ b/solution.py
@@ -98,10 +98,10 @@
 def whole_kernel(
     steps_ref, harm_ref, scale_ref, taps_ref, ridge_ref, out_ref,
     every, every_ridge, phase_ref,
-    colf, cols_s, rowf, rows_s, lowt, lowr, d0, d1, d2, e0, e1, e2, fcol, frow, mine, theirs, got_p,
+    colf, cols_s, rowf, rows_s, lowt, lowr, d0, d1, d2, e0, e1, e2, fcol, frow, mine, theirs, got_p, lead_own, lead_out, lead_in,
     la_ref, lb_ref, oa_ref, ob_ref, oc_ref,
     slab_a, slab_b, got_la, got_lb, got_oa, got_ob, ridge4, ridge_far, mat, nxt_ref,
-    s_st, r_st, s_ri, r_ri, s_p, r_p,
+    s_st, r_st, s_ri, r_ri, s_p, r_p, s_l, r_l,
     s_la, r_la, s_lb, r_lb, s_oa, r_oa, s_ob, r_ob, s_r, r_r, s_f, r_f,
     s_za, r_za, s_zb, r_zb, s_ca, r_ca, s_cb, r_cb,
 ):
@@ -151,8 +151,7 @@
     every_ridge[e] = ridge_ref[...]
     blocks = (ne * steps_ref.shape[1] // BLK) // (2 * NX)
     n_rows = rows_s.shape[0]
-    n_side = n_rows // 2
-    n_lead = n_side - 256
+    n_lead = (n_rows - 2 * B) // 2
     n_tiles = colf.shape[1] // 128
     cols_here = n_tiles - 2
     dcol, drow = (d0, d1, d2), (e0, e1, e2)
@@ -177,7 +176,7 @@
         cols_s[:, jt * 128 : jt * 128 + 128] = scale
     per = 128 // n_lead
     for side, gg in enumerate((group(z, 1 - core), g)):
-        top = side * n_side
+        top = 2 * n_lead + side * B
         for half in range(2):
             rows, scale = features(gg * 2 + half)
             at = slice(top + half * 128, top + half * 128 + 128)
@@ -185,7 +184,7 @@
             rows_s[at, :] = down(scale)
         rows, scale = features(gg // per)
         piece = pl.ds(pl.multiple_of((gg % per) * n_lead, n_lead), n_lead)
-        at = slice(top + 256, top + n_side)
+        at = slice(side * n_lead, side * n_lead + n_lead)
         lowr[...] = down(scale)
         rows_s[at, :] = lowr[piece, :]
         lowr[:, 0:16] = jnp.transpose(rows)
@@ -259,13 +258,13 @@
         both = jnp.concatenate(
             [dcol[s0][:, j0 : j0 + 256], dcol[s1][:, j0 : j0 + 256]], axis=0
         )
-        f = jnp.dot(low_up, both, preferred_element_type=F32)
-        fcol[pl.ds(pl.multiple_of(b * BLK, BLK), BLK), j0 : j0 + 256] = f.astype(BF16)
+        f = jnp.dot(low_up, both, preferred_element_type=F32).astype(BF16)
+        fcol[pl.ds(pl.multiple_of(b * BLK, BLK), BLK), j0 : j0 + 256] = f
 
     def filter_rows(b, s0, s1):
         both = jnp.concatenate([drow[s0][...], drow[s1][...]], axis=1)
-        f = jnp.dot(both, lowt[...], preferred_element_type=F32)
-        frow[:, pl.ds(pl.multiple_of(b * BLK, BLK), BLK)] = f.astype(BF16)
+        f = jnp.dot(both, lowt[...], preferred_element_type=F32).astype(BF16)
+        frow[:, pl.ds(pl.multiple_of(b * BLK, BLK), BLK)] = f
 
     wide = range(0, n_tiles * 128, 256)
     for b in range(2):
@@ -301,36 +300,48 @@
         block_pass(b, b % 3, b + 2 <= blocks)
 
     total = 1.0 / (blocks * BLK * 2 * NX)
+    leads, swaps = [], []
 
     def product(j):
         at = slice(j * B, j * B + B)
         part = jnp.dot(frow[...], fcol[:, at], preferred_element_type=F32) * total
-        theirs[j] = part[:n_side]
-        mine[j] = part[n_side:]
-        return put(theirs.at[j], got_p.at[j], s_p.at[j], r_p.at[j], other)
-
-    swaps = [product(0), product(1)]
-    swaps[0].wait()
-    part = mine[0] + got_p[0]
-    la_ref[...] = part[B:]
-    oa_ref[...] = part[:B].reshape(NX, 64, B)
+        lead_out[j] = part[:n_lead]
+        leads.append(put(lead_out.at[j], lead_in.at[j], s_l.at[j], r_l.at[j], other))
+        lead_own[j] = part[n_lead : 2 * n_lead]
+        theirs[j] = part[2 * n_lead : 2 * n_lead + B]
+        swaps.append(put(theirs.at[j], got_p.at[j], s_p.at[j], r_p.at[j], other))
+        mine[j] = part[2 * n_lead + B :]
+
+    own_piece = pl.ds(pl.multiple_of(x * 64, 64), 64)
+
+    def settle(j):
+        swaps[j].wait()
+        part = mine[j] + got_p[j]
+        if j == 0:
+            oa_ref[...] = part.reshape(NX, 64, B)
+            return
+        at = slice(j * B - B, j * B)
+        ob_ref[:, :, at] = part.astype(BF16).reshape(NX, 64, B)
+        oc_ref[:, at] = mine[j, own_piece, :] + got_p[j, own_piece, :]
+
+    product(0)
+    product(1)
+    leads[0].wait()
+    la_ref[...] = lead_own[0] + lead_in[0]
+    lead_a = to_x(lambda i: la_ref, got_la, s_la, r_la)
     ridge4[x] = every_ridge[0]
-    lead_a = to_x(lambda i: la_ref, got_la, s_la, r_la)
     ridges = [
         put(every_ridge.at[0], ridge4.at[x], s_r.at[i - 1], r_r.at[i - 1], peers[i - 1])
         for i in range(1, NX)
     ]
-    own_piece = pl.ds(pl.multiple_of(x * 64, 64), 64)
+    for j in range(2, n_tiles // 2):
+        product(j)
     for j in range(1, n_tiles // 2):
-        if j + 1 < n_tiles // 2:
-            swaps.append(product(j + 1))
-        swaps[j].wait()
-        part = mine[j] + got_p[j]
-        at = slice(j * B - B, j * B)
-        lb_ref[:, at] = part[B:]
-        ob_ref[:, :, at] = part[:B].astype(BF16).reshape(NX, 64, B)
-        oc_ref[:, at] = mine[j, own_piece, :] + got_p[j, own_piece, :]
+        leads[j].wait()
+        lb_ref[:, j * B - B : j * B] = lead_own[j] + lead_in[j]
     lead_b = to_x(lambda i: lb_ref, got_lb, s_lb, r_lb)
+    settle(0)
+    settle(1)
     for copy in lead_a:
         copy.wait()
     slab_a[g] = la_ref[...] + got_la[0] + got_la[1] + got_la[2]
@@ -339,6 +350,8 @@
     for copy in ridges:
         copy.wait()
     far = put(ridge4, ridge_far, s_f, r_f, device(x, (z + 4) % nz, core))
+    for j in range(2, n_tiles // 2):
+        settle(j)
     own_a = to_x(lambda i: oa_ref.at[(x + i) % NX], got_oa, s_oa, r_oa)
     own_b = to_x(lambda i: ob_ref.at[(x + i) % NX], got_ob, s_ob, r_ob)
     for copy in lead_b:
@@ -385,12 +398,13 @@
         nxt_ref[...] = pltpu.roll(mat[pl.ds(r1, NB), 0:B], B - r1, 1)[:, 0:128]
         return carry
 
-    half = B // NB // 2
-    lax.fori_loop(0, half, block_step, 0)
+    blocks_a = B // NB
+    early = blocks_a * 3 // 4
+    lax.fori_loop(0, early, block_step, 0)
     for i in range(1, nz):
         z_b[i - 1].wait()
         c_b.append(to_core(slab_b, s_cb, r_cb, i))
-    lax.fori_loop(half, 2 * half, block_step, 0)
+    lax.fori_loop(early, blocks_a, block_step, 0)
 
     for copy in own_a:
         copy.wait()
@@ -457,7 +471,8 @@
             *([vmem((n_rows, BLK), BF16)] * 3),
             vmem((here, width), BF16),
             vmem((n_rows, here), BF16),
-            *([vmem((width // B, n_rows // 2, B), F32)] * 3),
+            *([vmem((width // B, B, B), F32)] * 3),
+            *([vmem((width // B, 16, B), F32)] * 3),
             vmem((16, B), F32),
             vmem((16, cols), F32),
             vmem((NX, 64, B), F32),
@@ -473,7 +488,7 @@
             vmem((NX, 1, 64), F32),
             vmem((B, 2 * B), F32),
             vmem((NB, 128), F32),
-            *([dma((7,))] * 4), *([dma((5,))] * 2), *([dma((3,))] * 10), dma, dma,
+            *([dma((7,))] * 4), *([dma((5,))] * 4), *([dma((3,))] * 10), dma, dma,
             *([dma((7,))] * 4), *([dma((8,))] * 4),
         ],
         compiler_params=pltpu.CompilerParams(

time: 55.7 us -> 54.8 us (0.984)
  Pallas kernels: 54.9 us -> 54 us
    pallas_call x1, Pallas kernels: 53.2 us -> 52.3 us  [on_device(): pl.pallas_call(whole_kernel, out_shape=jax.ShapeDtypeStruct((64, width),...]
where the time goes in v7:
time: 54.8 us; the launch traced here: 54.6 us
  Pallas kernels  54 us (99%)
  between operations  0.64 us (1%)
    pallas_call x1, Pallas kernels, on_device(): pl.pallas_call(whole_kernel, out_shape=jax.ShapeDtypeStruct((64, width),...  52.3 us
    pallas_call x1, Pallas kernels, on_device(): pl.pallas_call(split_kernel, out_shape=(jax.ShapeDtypeStruct((64, B), F32...  1.7 us

profile of v7, /device:TPU:1, one launch (start us, length us, event | category | flops | bytes accessed | tf_op | source)
XLA Modules:
  0.0 54.6 jit_solution(14918426161015408571)
XLA Ops:
  0.6 52.3 %whole.1.both_ref = f32[64,1280]{1,0:T(8,128)} custom-call(s32[2,2048]{1,0:T(2,128)} %steps_ref.1, s32[32,128]{1,0:T(8,128)} %bitcast.4, f32[32,128]{1,0:T(8,128)} %bitcast.5, f32[2,128]{1,0:T(2,128)} %bitcast.6, f32[1,64]{1,0:T(1,128)} %bitcast.7), custom_call_target="tpu_custom_call" | custom-call | tf_op jit(solution)/shard_map/whole/pallas_call | solution.py:455
  52.9 1.7 %split.1 = (f32[64,256]{1,0:T(8,128)}, f32[64,1024]{1,0:T(8,128)}) custom-call(f32[64,1280]{1,0:T(8,128)} %whole.1.both_ref), custom_call_target="tpu_custom_call" | custom-call | tf_op jit(solution)/shard_map/split/pallas_call | solution.py:505

commit v8 on v7

--- a/solution.py
+++ b/solution.py
@@ -62,7 +62,7 @@
 NB = 32
 
 
-def block_inverse(a):
+def block_inverse(a, off):
     groups = NB // 8
     full = (8, 128)
     sub = lax.broadcasted_iota(jnp.int32, full, 0)
@@ -72,7 +72,7 @@
         return jnp.broadcast_to(v[s : s + 1, :], full)
 
     col = [
-        {k: jnp.broadcast_to(a[8 * k : 8 * k + 8, c : c + 1], full) for k in range(c // 8, groups)}
+        {k: jnp.broadcast_to(a[8 * k : 8 * k + 8, off + c : off + c + 1], full) for k in range(c // 8, groups)}
         for c in range(NB)
     ]
     inv = [jnp.where(lane == sub + 8 * k, 1.0, 0.0).astype(F32) for k in range(groups)]
@@ -97,10 +97,10 @@
 
 def whole_kernel(
     steps_ref, harm_ref, scale_ref, taps_ref, ridge_ref, out_ref,
-    every, every_ridge, phase_ref,
+    every, every_ridge, steps_out, phase_ref,
     colf, cols_s, rowf, rows_s, lowt, lowr, d0, d1, d2, e0, e1, e2, fcol, frow, mine, theirs, got_p, lead_own, lead_out, lead_in,
     la_ref, lb_ref, oa_ref, ob_ref, oc_ref,
-    slab_a, slab_b, got_la, got_lb, got_oa, got_ob, ridge4, ridge_far, mat, nxt_ref,
+    slab_a, slab_b, got_la, got_lb, got_oa, got_ob, ridge4, ridge_far, mat,
     s_st, r_st, s_ri, r_ri, s_p, r_p, s_l, r_l,
     s_la, r_la, s_lb, r_lb, s_oa, r_oa, s_ob, r_ob, s_r, r_r, s_f, r_f,
     s_za, r_za, s_zb, r_zb, s_ca, r_ca, s_cb, r_cb,
@@ -142,12 +142,13 @@
         k = group((z + nz - i) % nz, core)
         return put(slab.at[k], slab.at[k], send.at[i], recv.at[i], other)
 
+    steps_out[...] = steps_ref[...].astype(F32).astype(BF16)
     given = [
-        put(steps_ref, every.at[e], s_st.at[i], r_st.at[i], ring[i]) for i in range(ne - 1)
+        put(steps_out, every.at[e], s_st.at[i], r_st.at[i], ring[i]) for i in range(ne - 1)
     ] + [
         put(ridge_ref, every_ridge.at[e], s_ri.at[i], r_ri.at[i], ring[i]) for i in range(ne - 1)
     ]
-    every[e] = steps_ref[...]
+    every[e] = steps_out[...]
     every_ridge[e] = ridge_ref[...]
     blocks = (ne * steps_ref.shape[1] // BLK) // (2 * NX)
     n_rows = rows_s.shape[0]
@@ -378,33 +379,31 @@
         mat[64 * k : 64 * k + 64, 0:B] = rows + jnp.where(lane == sub + 64 * k, lead_ridge[k], 0.0)
         mat[64 * k : 64 * k + 64, B:] = jnp.where(lane == sub + 64 * k, 1.0, 0.0).astype(F32)
 
-    nxt_ref[...] = mat[0:NB, 0:128]
-    wide = lax.broadcasted_iota(jnp.int32, (NB, B), 1)
-
-    def block_step(j, carry):
-        r0 = pl.multiple_of(j * NB, NB)
+    turned = (((0,), (0,)), ((), ()))
+    following, off = mat[0:NB, 0:128], 0
+    for r0 in range(0, B, NB):
         r1 = r0 + NB
-        w = block_inverse(nxt_ref[:, 0:NB])[:, 0:NB]
-        rj = dot(w, mat[pl.ds(r0, NB), :])
-        mat[pl.ds(r0, NB), :] = rj
+        if r0 == B * 3 // 4:
+            for i in range(1, nz):
+                z_b[i - 1].wait()
+                c_b.append(to_core(slab_b, s_cb, r_cb, i))
+        w = block_inverse(following, off)[:, 0:NB]
+        if r1 == B:
+            mat[r0:r1, B:] = dot(w, mat[r0:r1, B:])
+            break
+        c0, w1 = r1 // 128 * 128, B + (r1 + 127) // 128 * 128
+        rj = dot(w, mat[r0:r1, c0:w1])
+        mat[r0:r1, B:w1] = rj[:, B - c0 :]
         hi, mid, low = split3(rj)
+        left = jnp.concatenate([hi, hi, mid, hi, low, mid], axis=0)
         right = jnp.concatenate([hi, mid, hi, low, hi, mid], axis=0)
-        hi, mid, low = split3(jnp.where(wide >= r1, rj[:, 0:B], 0.0))
-        left = jnp.concatenate([hi, hi, mid, hi, low, mid], axis=0)
-        mat[...] -= lax.dot_general(
-            left, right, (((0,), (0,)), ((), ())), preferred_element_type=F32
+        off = r1 - c0
+        near = lax.dot_general(
+            left[:, 0:128], right[:, 0:128], turned, preferred_element_type=F32
         )
-        r1 = pl.multiple_of(jnp.minimum(r1, B - NB), NB)
-        nxt_ref[...] = pltpu.roll(mat[pl.ds(r1, NB), 0:B], B - r1, 1)[:, 0:128]
-        return carry
-
-    blocks_a = B // NB
-    early = blocks_a * 3 // 4
-    lax.fori_loop(0, early, block_step, 0)
-    for i in range(1, nz):
-        z_b[i - 1].wait()
-        c_b.append(to_core(slab_b, s_cb, r_cb, i))
-    lax.fori_loop(early, blocks_a, block_step, 0)
+        following = mat[r1 : r1 + NB, c0 : c0 + 128] - near[off : off + NB, :]
+        step = lax.dot_general(left[:, : B - c0], right, turned, preferred_element_type=F32)
+        mat[r1:B, c0:w1] -= step[off:, :]
 
     for copy in own_a:
         copy.wait()
@@ -458,8 +457,9 @@
         in_specs=[VMEM] * 5,
         out_specs=VMEM,
         scratch_shapes=[
-            vmem((8, 2, steps.shape[1]), jnp.int32),
+            vmem((8, 2, steps.shape[1]), BF16),
             vmem((8, 1, 64), F32),
+            vmem((2, steps.shape[1]), BF16),
             vmem((256, 128), F32),
             vmem((16, width), BF16),
             vmem((1, width), F32),
@@ -487,7 +487,6 @@
             vmem((NX, 1, 64), F32),
             vmem((NX, 1, 64), F32),
             vmem((B, 2 * B), F32),
-            vmem((NB, 128), F32),
             *([dma((7,))] * 4), *([dma((5,))] * 4), *([dma((3,))] * 10), dma, dma,
             *([dma((7,))] * 4), *([dma((8,))] * 4),
         ],

time: 54.8 us -> 54 us (0.985)
  Pallas kernels: 54 us -> 53.2 us
    pallas_call x1, Pallas kernels: 52.3 us -> 51.5 us  [on_device(): pl.pallas_call(whole_kernel, out_shape=jax.ShapeDtypeStruct((64, width),...]
where the time goes in v8:
time: 54 us; the launch traced here: 53.8 us
  Pallas kernels  53.2 us (99%)
  between operations  0.64 us (1%)
    pallas_call x1, Pallas kernels, on_device(): pl.pallas_call(whole_kernel, out_shape=jax.ShapeDtypeStruct((64, width),...  51.5 us
    pallas_call x1, Pallas kernels, on_device(): pl.pallas_call(split_kernel, out_shape=(jax.ShapeDtypeStruct((64, B), F32...  1.7 us

profile of v8, /device:TPU:1, one launch (start us, length us, event | category | flops | bytes accessed | tf_op | source)
XLA Modules:
  0.0 53.8 jit_solution(5622818245578807904)
XLA Ops:
  0.6 51.5 %whole.1.both_ref = f32[64,1280]{1,0:T(8,128)} custom-call(s32[2,2048]{1,0:T(2,128)} %steps_ref.1, s32[32,128]{1,0:T(8,128)} %bitcast.4, f32[32,128]{1,0:T(8,128)} %bitcast.5, f32[2,128]{1,0:T(2,128)} %bitcast.6, f32[1,64]{1,0:T(1,128)} %bitcast.7), custom_call_target="tpu_custom_call" | custom-call | tf_op jit(solution)/shard_map/whole/pallas_call | solution.py:454
  52.1 1.7 %split.1 = (f32[64,256]{1,0:T(8,128)}, f32[64,1024]{1,0:T(8,128)}) custom-call(f32[64,1280]{1,0:T(8,128)} %whole.1.both_ref), custom_call_target="tpu_custom_call" | custom-call | tf_op jit(solution)/shard_map/split/pallas_call | solution.py:504

commit v9 on v8

--- a/solution.py
+++ b/solution.py
@@ -119,7 +119,8 @@
     across = [device(x, (1 - z // 4) * 4 + i, core) for i in range(4)]
     other = device(x, z, 1 - core)
     barrier = pltpu.get_barrier_semaphore()
-    greeted = ring + peers + across
+    cross = [device((x + i) % NX, z, 1 - core) for i in range(1, NX)]
+    greeted = ring + peers + cross + across
     for peer in greeted:
         pl.semaphore_signal(barrier, inc=1, device_id=peer, device_id_type=MESH)
     pl.semaphore_wait(barrier, len(greeted))
@@ -301,17 +302,21 @@
         block_pass(b, b % 3, b + 2 <= blocks)
 
     total = 1.0 / (blocks * BLK * 2 * NX)
-    leads, swaps = [], []
+    swaps = []
+
+    def leading(j):
+        part = jnp.dot(
+            frow[: 2 * n_lead, :], fcol[:, j * B : j * B + B], preferred_element_type=F32
+        )
+        return part[:n_lead] * total, part[n_lead:] * total
 
     def product(j):
-        at = slice(j * B, j * B + B)
-        part = jnp.dot(frow[...], fcol[:, at], preferred_element_type=F32) * total
-        lead_out[j] = part[:n_lead]
-        leads.append(put(lead_out.at[j], lead_in.at[j], s_l.at[j], r_l.at[j], other))
-        lead_own[j] = part[n_lead : 2 * n_lead]
-        theirs[j] = part[2 * n_lead : 2 * n_lead + B]
+        part = jnp.dot(
+            frow[2 * n_lead :, :], fcol[:, j * B : j * B + B], preferred_element_type=F32
+        )
+        theirs[j] = part[:B] * total
         swaps.append(put(theirs.at[j], got_p.at[j], s_p.at[j], r_p.at[j], other))
-        mine[j] = part[2 * n_lead + B :]
+        mine[j] = part[B:] * total
 
     own_piece = pl.ds(pl.multiple_of(x * 64, 64), 64)
 
@@ -325,41 +330,52 @@
         ob_ref[:, :, at] = part.astype(BF16).reshape(NX, 64, B)
         oc_ref[:, at] = mine[j, own_piece, :] + got_p[j, own_piece, :]
 
-    product(0)
-    product(1)
-    leads[0].wait()
-    la_ref[...] = lead_own[0] + lead_in[0]
-    lead_a = to_x(lambda i: la_ref, got_la, s_la, r_la)
+    given_a, own_a0 = leading(0)
+    la_ref[1 - core] = given_a
+    la_ref[core] = own_a0
+    lead_a = []
+    for i, peer in enumerate([other] + peers + cross):
+        side = core if 1 <= i < NX else 1 - core
+        lead_a.append(put(la_ref.at[side], got_la.at[i], s_la.at[i], r_la.at[i], peer))
     ridge4[x] = every_ridge[0]
     ridges = [
         put(every_ridge.at[0], ridge4.at[x], s_r.at[i - 1], r_r.at[i - 1], peers[i - 1])
         for i in range(1, NX)
     ]
-    for j in range(2, n_tiles // 2):
-        product(j)
     for j in range(1, n_tiles // 2):
-        leads[j].wait()
-        lb_ref[:, j * B - B : j * B] = lead_own[j] + lead_in[j]
+        at = slice(j * B - B, j * B)
+        lead_out[:, at], lead_own[:, at] = leading(j)
+    lead_swap = put(lead_out, lead_in, s_l, r_l, other)
+    product(0)
+    product(1)
+    lead_swap.wait()
+    lb_ref[...] = lead_own[...] + lead_in[...]
     lead_b = to_x(lambda i: lb_ref, got_lb, s_lb, r_lb)
-    settle(0)
-    settle(1)
+    product(2)
     for copy in lead_a:
         copy.wait()
-    slab_a[g] = la_ref[...] + got_la[0] + got_la[1] + got_la[2]
+    block = la_ref[core]
+    for i in range(2 * NX - 1):
+        block = block + got_la[i]
+    slab_a[g] = block
     z_a = to_z(slab_a, s_za, r_za)
     c_a = [to_core(slab_a, s_ca, r_ca, 0)]
     for copy in ridges:
         copy.wait()
     far = put(ridge4, ridge_far, s_f, r_f, device(x, (z + 4) % nz, core))
+    product(3)
+    settle(0)
+    product(4)
+    settle(1)
+    for copy in lead_b:
+        copy.wait()
+    slab_b[g] = (lb_ref[...] + got_lb[0] + got_lb[1] + got_lb[2]).astype(BF16)
+    z_b = to_z(slab_b, s_zb, r_zb)
+    c_b = [to_core(slab_b, s_cb, r_cb, 0)]
     for j in range(2, n_tiles // 2):
         settle(j)
     own_a = to_x(lambda i: oa_ref.at[(x + i) % NX], got_oa, s_oa, r_oa)
     own_b = to_x(lambda i: ob_ref.at[(x + i) % NX], got_ob, s_ob, r_ob)
-    for copy in lead_b:
-        copy.wait()
-    slab_b[g] = (lb_ref[...] + got_lb[0] + got_lb[1] + got_lb[2]).astype(BF16)
-    z_b = to_z(slab_b, s_zb, r_zb)
-    c_b = [to_core(slab_b, s_cb, r_cb, 0)]
     for i in range(1, nz):
         z_a[i - 1].wait()
         c_a.append(to_core(slab_a, s_ca, r_ca, i))
@@ -472,22 +488,22 @@
             vmem((here, width), BF16),
             vmem((n_rows, here), BF16),
             *([vmem((width // B, B, B), F32)] * 3),
-            *([vmem((width // B, 16, B), F32)] * 3),
-            vmem((16, B), F32),
+            *([vmem((16, cols), F32)] * 3),
+            vmem((2, 16, B), F32),
             vmem((16, cols), F32),
             vmem((NX, 64, B), F32),
             vmem((NX, 64, cols), BF16),
             vmem((64, cols), F32),
             vmem((16, 16, B), F32),
             vmem((16, 16, cols), BF16),
-            vmem((NX - 1, 16, B), F32),
+            vmem((2 * NX - 1, 16, B), F32),
             vmem((NX - 1, 16, cols), F32),
             vmem((NX - 1, 64, B), F32),
             vmem((NX - 1, 64, cols), BF16),
             vmem((NX, 1, 64), F32),
             vmem((NX, 1, 64), F32),
             vmem((B, 2 * B), F32),
-            *([dma((7,))] * 4), *([dma((5,))] * 4), *([dma((3,))] * 10), dma, dma,
+            *([dma((7,))] * 4), *([dma((5,))] * 2), dma, dma, *([dma((7,))] * 2), *([dma((3,))] * 8), dma, dma,
             *([dma((7,))] * 4), *([dma((8,))] * 4),
         ],
         compiler_params=pltpu.CompilerParams(

time: 54 us -> 50 us (0.926)
  Pallas kernels: 53.2 us -> 49.1 us
    pallas_call x1, Pallas kernels: 51.5 us -> 47.4 us  [on_device(): pl.pallas_call(whole_kernel, out_shape=jax.ShapeDtypeStruct((64, width),...]
where the time goes in v9:
time: 50 us; the launch traced here: 49.8 us
  Pallas kernels  49.1 us (98%)
  between operations  0.64 us (1%)
    pallas_call x1, Pallas kernels, on_device(): pl.pallas_call(whole_kernel, out_shape=jax.ShapeDtypeStruct((64, width),...  47.4 us
    pallas_call x1, Pallas kernels, on_device(): pl.pallas_call(split_kernel, out_shape=(jax.ShapeDtypeStruct((64, B), F32...  1.7 us

profile of v9, /device:TPU:1, one launch (start us, length us, event | category | flops | bytes accessed | tf_op | source)
XLA Modules:
  0.0 49.8 jit_solution(7289020223189538434)
XLA Ops:
  0.6 47.4 %whole.1.both_ref = f32[64,1280]{1,0:T(8,128)} custom-call(s32[2,2048]{1,0:T(2,128)} %steps_ref.1, s32[32,128]{1,0:T(8,128)} %bitcast.4, f32[32,128]{1,0:T(8,128)} %bitcast.5, f32[2,128]{1,0:T(2,128)} %bitcast.6, f32[1,64]{1,0:T(1,128)} %bitcast.7), custom_call_target="tpu_custom_call" | custom-call | tf_op jit(solution)/shard_map/whole/pallas_call | solution.py:470
  48.1 1.7 %split.1 = (f32[64,256]{1,0:T(8,128)}, f32[64,1024]{1,0:T(8,128)}) custom-call(f32[64,1280]{1,0:T(8,128)} %whole.1.both_ref), custom_call_target="tpu_custom_call" | custom-call | tf_op jit(solution)/shard_map/split/pallas_call | solution.py:520

commit v10 on v9

--- a/solution.py
+++ b/solution.py
@@ -16,6 +16,7 @@
 CHUNK = 64
 PERIOD = 4096
 NX = 4
+FAR_FIRST = (4, 3, 5, 2, 6, 1, 7)
 WAVE = (8.88573567404434, -58.45953046181323, 115.03267724691959, -100.39492606524867)
 ROUND = 12582912.0
 VMEM = pl.BlockSpec(memory_space=pltpu.VMEM)
@@ -96,7 +97,8 @@
 
 
 def whole_kernel(
-    steps_ref, harm_ref, scale_ref, taps_ref, ridge_ref, out_ref,
+    steps_hbm, harm_hbm, scale_hbm, taps_hbm, ridge_hbm, out_ref,
+    steps_ref, harm_ref, scale_ref, taps_ref, ridge_ref, s_in,
     every, every_ridge, steps_out, phase_ref,
     colf, cols_s, rowf, rows_s, lowt, lowr, d0, d1, d2, e0, e1, e2, fcol, frow, mine, theirs, got_p, lead_own, lead_out, lead_in,
     la_ref, lb_ref, oa_ref, ob_ref, oc_ref,
@@ -108,6 +110,13 @@
     x, y, z, core = place()
     e, p = lax.axis_index("epoch"), lax.axis_index("prow")
     nz, ne = 8, 8
+    fetches = []
+    for i, (src, dst) in enumerate((
+        (steps_hbm, steps_ref), (ridge_hbm, ridge_ref), (harm_hbm, harm_ref),
+        (scale_hbm, scale_ref), (taps_hbm, taps_ref),
+    )):
+        fetches.append(pltpu.make_async_copy(src, dst, s_in.at[i]))
+        fetches[-1].start()
 
     def group(zz, cc):
         return ((zz % 4) * 2 + cc) * 2 + zz // 4
@@ -124,6 +133,8 @@
     for peer in greeted:
         pl.semaphore_signal(barrier, inc=1, device_id=peer, device_id_type=MESH)
     pl.semaphore_wait(barrier, len(greeted))
+    for fetch in fetches:
+        fetch.wait()
 
     def put(src, dst, send, recv, peer):
         copy = pltpu.make_async_remote_copy(
@@ -137,7 +148,10 @@
         return [put(src(i), got.at[i - 1], send.at[i - 1], recv.at[i - 1], peers[i - 1]) for i in range(1, NX)]
 
     def to_z(slab, send, recv):
-        return [put(slab.at[g], slab.at[g], send.at[i - 1], recv.at[i - 1], tall[i - 1]) for i in range(1, nz)]
+        sent = {}
+        for i in FAR_FIRST:
+            sent[i - 1] = put(slab.at[g], slab.at[g], send.at[i - 1], recv.at[i - 1], tall[i - 1])
+        return sent
 
     def to_core(slab, send, recv, i):
         k = group((z + nz - i) % nz, core)
@@ -334,7 +348,9 @@
     la_ref[1 - core] = given_a
     la_ref[core] = own_a0
     lead_a = []
-    for i, peer in enumerate([other] + peers + cross):
+    row = [other] + peers + cross
+    for i in (2, 5, 1, 3, 4, 6, 0):
+        peer = row[i]
         side = core if 1 <= i < NX else 1 - core
         lead_a.append(put(la_ref.at[side], got_la.at[i], s_la.at[i], r_la.at[i], peer))
     ridge4[x] = every_ridge[0]
@@ -376,7 +392,7 @@
         settle(j)
     own_a = to_x(lambda i: oa_ref.at[(x + i) % NX], got_oa, s_oa, r_oa)
     own_b = to_x(lambda i: ob_ref.at[(x + i) % NX], got_ob, s_ob, r_ob)
-    for i in range(1, nz):
+    for i in reversed(FAR_FIRST):
         z_a[i - 1].wait()
         c_a.append(to_core(slab_a, s_ca, r_ca, i))
     far.wait()
@@ -400,7 +416,7 @@
     for r0 in range(0, B, NB):
         r1 = r0 + NB
         if r0 == B * 3 // 4:
-            for i in range(1, nz):
+            for i in reversed(FAR_FIRST):
                 z_b[i - 1].wait()
                 c_b.append(to_core(slab_b, s_cb, r_cb, i))
         w = block_inverse(following, off)[:, 0:NB]
@@ -470,9 +486,15 @@
     both = pl.pallas_call(
         whole_kernel,
         out_shape=jax.ShapeDtypeStruct((64, width), F32),
-        in_specs=[VMEM] * 5,
+        in_specs=[pl.BlockSpec(memory_space=pltpu.HBM)] * 5,
         out_specs=VMEM,
         scratch_shapes=[
+            vmem(steps.shape, jnp.int32),
+            vmem((32, 128), jnp.int32),
+            vmem((32, 128), F32),
+            vmem((2, 128), F32),
+            vmem((1, 64), F32),
+            dma((5,)),
             vmem((8, 2, steps.shape[1]), BF16),
             vmem((8, 1, 64), F32),
             vmem((2, steps.shape[1]), BF16),

time: 50 us -> 49.4 us (0.988)
  Pallas kernels: 49.1 us -> 48.6 us
where the time goes in v10:
time: 49.4 us; the launch traced here: 49.3 us
  Pallas kernels  48.6 us (98%)
  between operations  0.64 us (1%)
    pallas_call x1, Pallas kernels, on_device(): pl.pallas_call(whole_kernel, out_shape=jax.ShapeDtypeStruct((64, width),...  46.9 us
    pallas_call x1, Pallas kernels, on_device(): pl.pallas_call(split_kernel, out_shape=(jax.ShapeDtypeStruct((64, B), F32...  1.7 us

profile of v10, /device:TPU:1, one launch (start us, length us, event | category | flops | bytes accessed | tf_op | source)
XLA Modules:
  0.0 49.3 jit_solution(16500224117567433770)
XLA Ops:
  0.6 46.9 %whole.1.both_ref = f32[64,1280]{1,0:T(8,128)} custom-call(s32[2,2048]{1,0:T(2,128)} %steps_hbm.1, s32[32,128]{1,0:T(8,128)} %bitcast.4, f32[32,128]{1,0:T(8,128)} %bitcast.5, f32[2,128]{1,0:T(2,128)} %bitcast.6, f32[1,64]{1,0:T(1,128)} %bitcast.7), custom_call_target="tpu_custom_call" | custom-call | tf_op jit(solution)/shard_map/whole/pallas_call | solution.py:486
  47.6 1.7 %split.1 = (f32[64,256]{1,0:T(8,128)}, f32[64,1024]{1,0:T(8,128)}) custom-call(f32[64,1280]{1,0:T(8,128)} %whole.1.both_ref), custom_call_target="tpu_custom_call" | custom-call | tf_op jit(solution)/shard_map/split/pallas_call | solution.py:542

commit v11 on v10

--- a/solution.py
+++ b/solution.py
@@ -396,8 +396,6 @@
         z_a[i - 1].wait()
         c_a.append(to_core(slab_a, s_ca, r_ca, i))
     far.wait()
-    for copy in c_a:
-        copy.wait()
 
     lane = lax.broadcasted_iota(jnp.int32, (64, B), 1)
     sub = lax.broadcasted_iota(jnp.int32, (64, B), 0)
@@ -406,10 +404,13 @@
         return jnp.transpose(jnp.broadcast_to(row, (128, 64)))[:, 0:1]
 
     lead_ridge = [column(jnp.where(z < 4, ridge4[k], ridge_far[k])) for k in range(4)]
+    for k in range(4):
+        mat[64 * k : 64 * k + 64, B:] = jnp.where(lane == sub + 64 * k, 1.0, 0.0).astype(F32)
+    for copy in c_a:
+        copy.wait()
     for k in range(4):
         rows = slab_a[4 * k : 4 * k + 4].reshape(64, B)
         mat[64 * k : 64 * k + 64, 0:B] = rows + jnp.where(lane == sub + 64 * k, lead_ridge[k], 0.0)
-        mat[64 * k : 64 * k + 64, B:] = jnp.where(lane == sub + 64 * k, 1.0, 0.0).astype(F32)
 
     turned = (((0,), (0,)), ((), ()))
     following, off = mat[0:NB, 0:128], 0

time: 49.4 us -> 49.4 us (level)
  no operation moved by 1% of the time
where the time goes in v11:
time: 49.4 us; the launch traced here: 49.3 us
  Pallas kernels  48.6 us (98%)
  between operations  0.64 us (1%)
    pallas_call x1, Pallas kernels, on_device(): pl.pallas_call(whole_kernel, out_shape=jax.ShapeDtypeStruct((64, width),...  46.9 us
    pallas_call x1, Pallas kernels, on_device(): pl.pallas_call(split_kernel, out_shape=(jax.ShapeDtypeStruct((64, B), F32...  1.7 us

profile of v11, /device:TPU:1, one launch (start us, length us, event | category | flops | bytes accessed | tf_op | source)
XLA Modules:
  0.0 49.3 jit_solution(6978190907138298146)
XLA Ops:
  0.6 46.9 %whole.1.both_ref = f32[64,1280]{1,0:T(8,128)} custom-call(s32[2,2048]{1,0:T(2,128)} %steps_hbm.1, s32[32,128]{1,0:T(8,128)} %bitcast.4, f32[32,128]{1,0:T(8,128)} %bitcast.5, f32[2,128]{1,0:T(2,128)} %bitcast.6, f32[1,64]{1,0:T(1,128)} %bitcast.7), custom_call_target="tpu_custom_call" | custom-call | tf_op jit(solution)/shard_map/whole/pallas_call | solution.py:487
  47.6 1.7 %split.1 = (f32[64,256]{1,0:T(8,128)}, f32[64,1024]{1,0:T(8,128)}) custom-call(f32[64,1280]{1,0:T(8,128)} %whole.1.both_ref), custom_call_target="tpu_custom_call" | custom-call | tf_op jit(solution)/shard_map/split/pallas_call | solution.py:543
